TPU v7x, 32 devices: a whole 2x2x4 slice. The times are simulated.
32 devices in a mesh: segment: 2 (over x), seq: 4 (over y, core), head: 4 (over z).
Axes of the slice: x: 2, y: 2, z: 4, core: 2. Of those that a mesh axis runs over, the one named last changes fastest.
Arguments:
- stream: bfloat16 [2, 512, 4096], P(None, 'seq', 'head'), may hold values from -6 to 6
- in_gain: float32 [2, 4096], P('segment'), may hold values from 0.25 to 1.75
- w_qkv: bfloat16 [2, 4096, 4, 3, 512], P('segment', None, 'head'), may hold values from -0.09375 to 0.09375
- qk_gain: float32 [2, 4, 2, 512], P('segment', 'head'), may hold values from 0.25 to 1.75
- w_one: bfloat16 [2, 4, 512, 768], P('segment', 'head'), may hold values from -0.25 to 0.25
- w_three: bfloat16 [2, 4, 512, 768], P('segment', 'head'), may hold values from -0.25 to 0.25
- w_two: bfloat16 [2, 4, 768, 512], P('segment', 'head'), may hold values from -0.21875 to 0.21875
- token_rate: float32 [2, 2, 512], P('segment', None, 'seq'), may hold values from 0.05 to 1
- out_gain: float32 [2, 4, 512], P('segment', 'head'), may hold values from 0.25 to 1.75
- w_out: bfloat16 [2, 4, 512, 4096], P('segment', 'head'), may hold values from -0.125 to 0.125
Outputs:
- sections_out: bfloat16 [2, 2, 512, 4096], P('segment', None, 'seq', 'head')
All inputs are finite; a program needn't handle non-finite values.
Results may differ from a plain program's by a relative error of at most 0.038.
Values may be sent and summed in bfloat16 or wider, within the bound.
A program may use at most 128 MiB of HBM per device.

v0:
```python
import jax
import jax.numpy as jnp
from jax import lax
from jax.sharding import PartitionSpec as P

NS_STEPS = 2


ns_first = 3.4445
ns_second = -4.775
ns_third = 2.0315
update_step = 1.0
norm_eps = 1e-06
grad_eps = 1e-07


def shifted(array, axis, by):
    devices = lax.axis_size(axis)
    pairs = [(i, i + by) for i in range(devices) if 0 <= i + by < devices]
    return lax.ppermute(array, axis, pairs)


def rms_scale(values):
    return values * lax.rsqrt(jnp.mean(values * values, axis=-1, keepdims=True) + norm_eps)


def contract_rows(left, right):
    return lax.dot_general(
        left, right, (((0,), (0,)), ((), ())), preferred_element_type=jnp.float32
    )


def renormalize(weights, target_norms):
    return weights * (target_norms / (jnp.sqrt(jnp.sum(weights * weights, axis=0)) + norm_eps))


def orthogonal_updates(shares):
    squares = jnp.stack([jnp.sum(share * share) for share in shares])
    totals = lax.psum(squares, "seq")
    current = [
        (shares[index] / (jnp.sqrt(totals[index]) + grad_eps)).astype(jnp.bfloat16)
        for index in range(3)
    ]
    for sweep_index in range(NS_STEPS):
        partial_grams = jnp.stack(
            [
                lax.dot_general(
                    block, block, (((1,), (1,)), ((), ())), preferred_element_type=jnp.float32
                )
                .astype(jnp.bfloat16)
                .astype(jnp.float32)
                for block in current
            ]
        )
        grams = lax.psum(partial_grams.astype(jnp.bfloat16), "seq")
        following = []
        for index in range(3):
            gram_matrix = grams[index]
            square = jnp.dot(gram_matrix, gram_matrix, preferred_element_type=jnp.float32)
            mixing = (ns_second * gram_matrix.astype(jnp.float32) + ns_third * square).astype(
                jnp.bfloat16
            )
            block = current[index]
            following.append(
                (
                    ns_first * block.astype(jnp.float32)
                    + jnp.dot(mixing, block, preferred_element_type=jnp.float32)
                ).astype(jnp.bfloat16)
            )
        current = following
    return (
        lax.all_gather(current[0], "seq", axis=1, tiled=True),
        lax.all_gather(current[1], "seq", axis=1, tiled=True),
        lax.all_gather(current[2], "seq", axis=1, tiled=True),
    )


def run_section(
    residual, gain_row, qkv_matrix, head_gains, rate_row, out_gain_row, out_weights, fasts, norms
):
    values = residual.astype(jnp.float32)
    head_width = head_gains.shape[-1]
    whole = lax.all_gather(residual, "head", axis=1, tiled=True)
    normed = (rms_scale(whole.astype(jnp.float32)) * gain_row).astype(jnp.bfloat16)
    projected = jnp.dot(normed, qkv_matrix, preferred_element_type=jnp.float32)
    projected = projected.reshape(residual.shape[0], 3, head_width)
    queries = rms_scale(projected[:, 0]) * head_gains[0]
    key_rows = (rms_scale(projected[:, 1]) * head_gains[1]).astype(jnp.bfloat16)
    out_grad = (-rate_row[:, None] * projected[:, 2]).astype(jnp.bfloat16)
    gate_fast, up_fast, down_fast = fasts
    gate_low = gate_fast.astype(jnp.bfloat16)
    up_low = up_fast.astype(jnp.bfloat16)
    down_low = down_fast.astype(jnp.bfloat16)
    pre_gate = jnp.dot(key_rows, gate_low, preferred_element_type=jnp.float32)
    pre_up = jnp.dot(key_rows, up_low, preferred_element_type=jnp.float32)
    sigmoid_gate = jax.nn.sigmoid(pre_gate)
    gated = pre_gate * sigmoid_gate
    hidden = (gated * pre_up).astype(jnp.bfloat16)
    backward = lax.dot_general(
        out_grad, down_low, (((1,), (1,)), ((), ())), preferred_element_type=jnp.float32
    )
    grad_gate = (backward * pre_up * sigmoid_gate * (1.0 + pre_gate * (1.0 - sigmoid_gate))).astype(
        jnp.bfloat16
    )
    grad_up = (backward * gated).astype(jnp.bfloat16)
    all_keys, all_grads = (
        lax.all_gather(key_rows, "seq", axis=0, tiled=True),
        lax.all_gather(out_grad, "seq", axis=0, tiled=True),
    )
    hidden_part, gate_part, up_part = (
        lax.all_to_all(hidden, "seq", split_axis=1, concat_axis=0, tiled=True),
        lax.all_to_all(grad_gate, "seq", split_axis=1, concat_axis=0, tiled=True),
        lax.all_to_all(grad_up, "seq", split_axis=1, concat_axis=0, tiled=True),
    )
    shares = (
        contract_rows(all_keys, gate_part),
        contract_rows(all_keys, up_part),
        contract_rows(all_grads, hidden_part),
    )
    gate_step, up_step, down_step = orthogonal_updates(shares)
    gate_fast = renormalize(gate_fast - update_step * gate_step.astype(jnp.float32), norms[0])
    up_fast = renormalize(up_fast - update_step * up_step.astype(jnp.float32), norms[1])
    down_fast = renormalize(down_fast - update_step * down_step.astype(jnp.float32).T, norms[2])
    gate_out = jnp.dot(queries, gate_fast, precision=lax.Precision.HIGHEST)
    up_out = jnp.dot(queries, up_fast, precision=lax.Precision.HIGHEST)
    output = jnp.dot(jax.nn.silu(gate_out) * up_out, down_fast, precision=lax.Precision.HIGHEST)
    normed_out = (rms_scale(output) * out_gain_row).astype(jnp.bfloat16)
    head_terms = jnp.dot(normed_out, out_weights, preferred_element_type=jnp.float32)
    delta = lax.psum_scatter(
        head_terms.astype(jnp.bfloat16), "head", scatter_dimension=1, tiled=True
    ).astype(jnp.float32)
    return ((values + delta).astype(jnp.bfloat16), (gate_fast, up_fast, down_fast))


def shards(stream, in_gain, w_qkv, qk_gain, w_one, w_three, w_two, token_rate, out_gain, w_out):
    segment_index = lax.axis_index("segment")
    span_count = stream.shape[0]
    moments = span_count + lax.axis_size("segment") - 1
    qkv_matrix = w_qkv[0].reshape(w_qkv.shape[1], -1)
    fasts = (
        w_one[0, 0].astype(jnp.float32),
        w_three[0, 0].astype(jnp.float32),
        w_two[0, 0].astype(jnp.float32),
    )
    norms = tuple((jnp.sqrt(jnp.sum(matrix * matrix, axis=0)) for matrix in fasts))
    received = jnp.zeros_like(stream[0])
    collected = jnp.zeros(stream.shape, jnp.bfloat16)
    for moment in range(moments):
        span_index = moment - segment_index
        active = (span_index >= 0) & (span_index < span_count)
        clipped = jnp.clip(span_index, 0, span_count - 1)
        source = jnp.where(segment_index == 0, stream[min(moment, span_count - 1)], received)
        rate_row = lax.dynamic_index_in_dim(token_rate[0], clipped, 0, keepdims=False)
        result, updated = run_section(
            source,
            in_gain[0],
            qkv_matrix,
            qk_gain[0, 0],
            rate_row,
            out_gain[0, 0],
            w_out[0, 0],
            fasts,
            norms,
        )
        fasts = tuple((jnp.where(active, fresh, former) for fresh, former in zip(updated, fasts)))
        chosen = jnp.arange(span_count) == span_index
        collected = jnp.where(chosen[:, None, None], result[None], collected)
        if moment + 1 < moments:
            received = shifted(result, "segment", 1)
    return collected[None]


def solution(mesh):
    placed = (
        P(None, "seq", "head"),
        P("segment", None),
        P("segment", None, "head", None, None),
        P("segment", "head", None, None),
        P("segment", "head", None, None),
        P("segment", "head", None, None),
        P("segment", "head", None, None),
        P("segment", None, "seq"),
        P("segment", "head", None),
        P("segment", "head", None, None),
    )
    return jax.shard_map(
        shards,
        mesh=mesh,
        in_specs=placed,
        out_specs=P("segment", None, "seq", "head"),
        check_vma=False,
    )
```

profile of v0, /device:TPU:0, one launch (start us, length us, event | category | flops | bytes accessed | tf_op | source)
XLA Modules:
  0.0 861.6 jit_solution(11526859129735552482)
XLA Ops:
  8.3 17.0 %copy.13 = bf16[1,4096,1,3,512]{1,4,3,2,0:T(8,128)(2,1)} copy(bf16[1,4096,1,3,512]{4,1,3,2,0:T(8,128)(2,1)} %param.12) | data formatting | bytes 25165824 | tf_op args[2]
  26.4 13.3 %all-gather.9.cloned.1.call-done = bf16[1,128,4096]{2,1,0:T(8,128)(2,1)} async-done(((bf16[1,128,1024]{2,1,0:T(8,128)(2,1)}), bf16[1,128,4096]{2,1,0:T(8,128)(2,1)}) %all-gather.9.cloned.1.call-update) | async-done | bytes 1048592 | tf_op jit(solution)/shard_map/all_gather | solution.py:83
  41.3 8.9 %fusion.4 = f32[128,3,512]{2,0,1:T(8,128)S(1)} fusion(bf16[1,4096,1,3,512]{1,4,3,2,0:T(8,128)(2,1)} %copy.13, bf16[1,128,4096]{2,1,0:T(8,128)(2,1)S(1)} %copy-done.31, f32[4096]{0:T(1024)S(1)} %bitcast.605, f32[128]{0:T(128)S(1)} %add_rsqrt_fusion.11), kind=kOutput, calls=%fused_computation.4 | convolution fusion | flops 1612709888 | bytes 14434816 | tf_op jit(solution)/shard_map/dot_general | solution.py:85
  58.3 8.9 %all_gather.55 = bf16[512,512]{1,0:T(8,128)(2,1)S(1)} all-gather(bf16[128,512]{1,0:T(8,128)(2,1)S(1)} %get-tuple-element.30), channel_id=1, replica_groups=mesh['segment'=2,'seq'=4,'head'=4] {'seq'}, dimensions={0}, use_global_device_ids=true | all-gather | bytes 655360 | tf_op jit(solution)/shard_map/all_gather | solution.py:107
  68.9 7.3 all_gather.56
  108.2 41.7 %all-reduce.7.cloned.1.call-done = bf16[3,512,512]{2,1,0:T(8,128)(2,1)} async-done(((bf16[3,512,512]{2,1,0:T(8,128)(2,1)}), bf16[3,512,512]{2,1,0:T(8,128)(2,1)}) %all-reduce.7.cloned.1.call-update) | async-done | bytes 1572880 | tf_op jit(solution)/shard_map/psum | solution.py:55
  162.1 39.8 %all-reduce.9.cloned.1.call-done = bf16[3,512,512]{2,1,0:T(8,128)(2,1)} async-done(((bf16[3,512,512]{2,1,0:T(8,128)(2,1)}), bf16[3,512,512]{2,1,0:T(8,128)(2,1)}) %all-reduce.9.cloned.1.call-update) | async-done | bytes 1572880 | tf_op jit(solution)/shard_map/psum | solution.py:55
  204.0 8.3 all_gather.59
  215.4 8.7 %all_gather.57 = bf16[512,768]{0,1:T(8,128)(2,1)S(1)} all-gather(bf16[512,192]{0,1:T(8,128)(2,1)S(1)} %fusion.155), channel_id=1, replica_groups=mesh['segment'=2,'seq'=4,'head'=4] {'seq'}, dimensions={1}, use_global_device_ids=true | all-gather | bytes 983040 | tf_op jit(solution)/shard_map/all_gather | solution.py:72
  226.4 8.8 %all_gather.58 = bf16[512,768]{0,1:T(8,128)(2,1)S(1)} all-gather(bf16[512,192]{0,1:T(8,128)(2,1)S(1)} %fusion.154), channel_id=1, replica_groups=mesh['segment'=2,'seq'=4,'head'=4] {'seq'}, dimensions={1}, use_global_device_ids=true | all-gather | bytes 983040 | tf_op jit(solution)/shard_map/all_gather | solution.py:73
  244.5 27.9 %reduce-scatter.4.cloned.1.call-done = bf16[128,1024]{1,0:T(8,128)(2,1)} async-done(((bf16[128,4096]{1,0:T(8,128)(2,1)}), bf16[128,1024]{1,0:T(8,128)(2,1)}) %reduce-scatter.4.cloned.1.call-update) | async-done | bytes 262160 | tf_op jit(solution)/shard_map/reduce_scatter | solution.py:129
  284.4 28.0 %all-gather.5.cloned.1.call-done = bf16[128,4096]{1,0:T(8,128)(2,1)} async-done(((bf16[128,1024]{1,0:T(8,128)(2,1)}), bf16[128,4096]{1,0:T(8,128)(2,1)}) %all-gather.5.cloned.1.call-update) | async-done | bytes 1048592 | tf_op jit(solution)/shard_map/all_gather | solution.py:83
  314.1 8.9 %fusion.2 = f32[128,3,512]{2,0,1:T(8,128)S(1)} fusion(bf16[1,4096,1,3,512]{1,4,3,2,0:T(8,128)(2,1)} %copy.13, bf16[128,4096]{1,0:T(8,128)(2,1)S(1)} %copy-done.33, f32[128]{0:T(128)S(1)} %add_rsqrt_fusion.7, f32[4096]{0:T(1024)S(1)} %bitcast.606), kind=kOutput, calls=%fused_computation.2 | convolution fusion | flops 1612709888 | bytes 14434816 | tf_op jit(solution)/shard_map/dot_general | solution.py:85
  323.7 8.0 all_gather.61
  342.0 8.1 all_gather.62
  372.7 6.4 psum.66
  386.1 41.7 %all-reduce.11.cloned.1.call-done = bf16[3,512,512]{2,1,0:T(8,128)(2,1)} async-done(((bf16[3,512,512]{2,1,0:T(8,128)(2,1)}), bf16[3,512,512]{2,1,0:T(8,128)(2,1)}) %all-reduce.11.cloned.1.call-update) | async-done | bytes 1572880 | tf_op jit(solution)/shard_map/psum | solution.py:55
  441.9 41.9 %all-reduce.13.cloned.1.call-done = bf16[3,512,512]{2,1,0:T(8,128)(2,1)} async-done(((bf16[3,512,512]{2,1,0:T(8,128)(2,1)}), bf16[3,512,512]{2,1,0:T(8,128)(2,1)}) %all-reduce.13.cloned.1.call-update) | async-done | bytes 1572880 | tf_op jit(solution)/shard_map/psum | solution.py:55
  486.8 8.4 all_gather.65
  500.8 9.0 %all_gather.63 = bf16[512,768]{0,1:T(8,128)(2,1)S(1)} all-gather(bf16[512,192]{0,1:T(8,128)(2,1)} %fusion.149), channel_id=1, replica_groups=mesh['segment'=2,'seq'=4,'head'=4] {'seq'}, dimensions={1}, use_global_device_ids=true | all-gather | bytes 983040 | tf_op jit(solution)/shard_map/all_gather | solution.py:72
  515.2 9.0 %all_gather.64 = bf16[512,768]{0,1:T(8,128)(2,1)S(1)} all-gather(bf16[512,192]{0,1:T(8,128)(2,1)S(1)} %fusion.148), channel_id=1, replica_groups=mesh['segment'=2,'seq'=4,'head'=4] {'seq'}, dimensions={1}, use_global_device_ids=true | all-gather | bytes 983040 | tf_op jit(solution)/shard_map/all_gather | solution.py:73
  534.4 27.9 %reduce-scatter.6.cloned.1.call-done = bf16[128,1024]{1,0:T(8,128)(2,1)} async-done(((bf16[128,4096]{1,0:T(8,128)(2,1)}), bf16[128,1024]{1,0:T(8,128)(2,1)}) %reduce-scatter.6.cloned.1.call-update) | async-done | bytes 262160 | tf_op jit(solution)/shard_map/reduce_scatter | solution.py:129
  574.3 28.0 %all-gather.7.cloned.1.call-done = bf16[128,4096]{1,0:T(8,128)(2,1)} async-done(((bf16[128,1024]{1,0:T(8,128)(2,1)}), bf16[128,4096]{1,0:T(8,128)(2,1)}) %all-gather.7.cloned.1.call-update) | async-done | bytes 1048592 | tf_op jit(solution)/shard_map/all_gather | solution.py:83
  603.9 9.0 %fusion = f32[128,3,512]{2,0,1:T(8,128)S(1)} fusion(bf16[1,4096,1,3,512]{1,4,3,2,0:T(8,128)(2,1)} %copy.13, bf16[128,4096]{1,0:T(8,128)(2,1)S(1)} %copy-done.32, f32[128]{0:T(128)S(1)} %add_rsqrt_fusion.3, f32[4096]{0:T(1024)S(1)} %bitcast.607), kind=kOutput, calls=%fused_computation | convolution fusion | flops 1612709888 | bytes 14434816 | tf_op jit(solution)/shard_map/dot_general | solution.py:85
  613.2 7.9 all_gather.67
  632.8 8.1 all_gather.68
  674.9 41.7 %all-reduce.15.cloned.1.call-done = bf16[3,512,512]{2,1,0:T(8,128)(2,1)} async-done(((bf16[3,512,512]{2,1,0:T(8,128)(2,1)}), bf16[3,512,512]{2,1,0:T(8,128)(2,1)}) %all-reduce.15.cloned.1.call-update) | async-done | bytes 1572880 | tf_op jit(solution)/shard_map/psum | solution.py:55
  730.1 42.4 %all-reduce.17.cloned.1.call-done = bf16[3,512,512]{2,1,0:T(8,128)(2,1)} async-done(((bf16[3,512,512]{2,1,0:T(8,128)(2,1)}), bf16[3,512,512]{2,1,0:T(8,128)(2,1)}) %all-reduce.17.cloned.1.call-update) | async-done | bytes 1572880 | tf_op jit(solution)/shard_map/psum | solution.py:55
  775.5 8.3 all_gather.71
  789.4 8.9 %all_gather.69 = bf16[512,768]{0,1:T(8,128)(2,1)S(1)} all-gather(bf16[512,192]{0,1:T(8,128)(2,1)} %fusion.143), channel_id=1, replica_groups=mesh['segment'=2,'seq'=4,'head'=4] {'seq'}, dimensions={1}, use_global_device_ids=true | all-gather | bytes 983040 | tf_op jit(solution)/shard_map/all_gather | solution.py:72
  803.6 9.0 %all_gather.70 = bf16[512,768]{0,1:T(8,128)(2,1)S(1)} all-gather(bf16[512,192]{0,1:T(8,128)(2,1)S(1)} %fusion.142), channel_id=1, replica_groups=mesh['segment'=2,'seq'=4,'head'=4] {'seq'}, dimensions={1}, use_global_device_ids=true | all-gather | bytes 983040 | tf_op jit(solution)/shard_map/all_gather | solution.py:73
  824.4 27.9 %reduce-scatter.8.cloned.1.call-done = bf16[128,1024]{1,0:T(8,128)(2,1)} async-done(((bf16[128,4096]{1,0:T(8,128)(2,1)}), bf16[128,1024]{1,0:T(8,128)(2,1)}) %reduce-scatter.8.cloned.1.call-update) | async-done | bytes 262160 | tf_op jit(solution)/shard_map/reduce_scatter | solution.py:129
  (391 shorter events, 260.8 us)
Async XLA Ops:
  6.5 33.1 %all-gather.9.cloned.1.call-start = ((), (), s32[]{:S(2)}) async-start(), calls=%async_computation.23 | async-start | bytes 1310720 | tf_op jit(solution)/shard_map/all_gather | solution.py:83
  8.3 33.0 %copy-start.57 = (f32[1,4096]{1,0:T(1,128)S(1)}, f32[1,4096]{1,0:T(1,128)}, u32[]{:S(2)}) copy-start(f32[1,4096]{1,0:T(1,128)} %param.11) | copy-start | bytes 49156
  54.9 21.2 %all-to-all-start = ((bf16[128,4,192]{0,2,1:T(8,128)(2,1)}), bf16[128,4,192]{0,2,1:T(8,128)(2,1)S(1)}, u32[]{:S(2)}, u32[]{:S(2)}) async-start(bf16[128,4,192]{0,2,1:T(8,128)(2,1)} %bitcast.19), calls=%async_computation | async-start | bytes 393216 | tf_op jit(solution)/shard_map/all_to_all | solution.py:112
  76.1 8.6 %all-to-all-start.1 = ((bf16[128,4,192]{0,2,1:T(8,128)(2,1)}), bf16[128,4,192]{0,2,1:T(8,128)(2,1)S(1)}, u32[]{:S(2)}, u32[]{:S(2)}) async-start(bf16[128,4,192]{0,2,1:T(8,128)(2,1)} %bitcast.22), calls=%async_computation.1 | async-start | bytes 393216 | tf_op jit(solution)/shard_map/all_to_all | solution.py:113
  84.8 8.6 %all-to-all-start.2 = ((bf16[128,4,192]{0,2,1:T(8,128)(2,1)}), bf16[128,4,192]{0,2,1:T(8,128)(2,1)S(1)}, u32[]{:S(2)}, u32[]{:S(2)}) async-start(bf16[128,4,192]{0,2,1:T(8,128)(2,1)} %bitcast.26), calls=%async_computation.2 | async-start | bytes 393216 | tf_op jit(solution)/shard_map/all_to_all | solution.py:111
  88.2 61.7 %all-reduce.7.cloned.1.call-start = ((), (), s32[]{:S(2)}) async-start(), calls=%async_computation.12 | async-start | bytes 3145728 | tf_op jit(solution)/shard_map/psum | solution.py:55
  108.2 44.2 %copy-start.55 = (f32[512,192]{0,1:T(8,128)S(1)}, f32[512,192]{0,1:T(8,128)}, u32[]{:S(2)}) copy-start(f32[512,192]{0,1:T(8,128)} %get-tuple-element.47) | copy-start | bytes 1179652
  108.2 93.7 %all-reduce.9.cloned.1.call-start = ((), (), s32[]{:S(2)}) async-start(), calls=%async_computation.13 | async-start | bytes 3145728 | tf_op jit(solution)/shard_map/psum | solution.py:55
  158.8 113.6 %reduce-scatter.4.cloned.1.call-start = ((), (), s32[]{:S(2)}) async-start(), calls=%async_computation.14 | async-start | bytes 1310720 | tf_op jit(solution)/shard_map/reduce_scatter | solution.py:129
  236.0 96.4 %copy-start.75 = (f32[512]{0:T(512)}, f32[512]{0:T(512)S(1)}, u32[]{:S(2)}) copy-start(f32[512]{0:T(512)S(1)} %add_divide_fusion.11) | copy-start | bytes 6148
  237.1 95.8 %copy-start.58 = (f32[768]{0:T(1024)}, f32[768]{0:T(1024)S(1)}, u32[]{:S(2)}) copy-start(f32[768]{0:T(1024)S(1)} %add_divide_fusion.8) | copy-start | bytes 9220
  237.5 94.2 %copy-start.70 = (f32[768]{0:T(1024)}, f32[768]{0:T(1024)S(1)}, u32[]{:S(2)}) copy-start(f32[768]{0:T(1024)S(1)} %add_divide_fusion.7) | copy-start | bytes 9220
  244.5 67.9 %all-gather.5.cloned.1.call-start = ((), (), s32[]{:S(2)}) async-start(), calls=%async_computation.15 | async-start | bytes 1310720 | tf_op jit(solution)/shard_map/all_gather | solution.py:83
  274.2 8.5 collective-permute-start
  335.2 15.0 %all-to-all-start.3 = ((bf16[128,4,192]{0,2,1:T(8,128)(2,1)}), bf16[128,4,192]{0,2,1:T(8,128)(2,1)S(1)}, u32[]{:S(2)}, u32[]{:S(2)}) async-start(bf16[128,4,192]{0,2,1:T(8,128)(2,1)} %bitcast.54), calls=%async_computation.4 | async-start | bytes 393216 | tf_op jit(solution)/shard_map/all_to_all | solution.py:112
  350.1 8.6 %all-to-all-start.4 = ((bf16[128,4,192]{0,2,1:T(8,128)(2,1)}), bf16[128,4,192]{0,2,1:T(8,128)(2,1)S(1)}, u32[]{:S(2)}, u32[]{:S(2)}) async-start(bf16[128,4,192]{0,2,1:T(8,128)(2,1)} %bitcast.57), calls=%async_computation.5 | async-start | bytes 393216 | tf_op jit(solution)/shard_map/all_to_all | solution.py:113
  358.8 8.6 %all-to-all-start.5 = ((bf16[128,4,192]{0,2,1:T(8,128)(2,1)}), bf16[128,4,192]{0,2,1:T(8,128)(2,1)S(1)}, u32[]{:S(2)}, u32[]{:S(2)}) async-start(bf16[128,4,192]{0,2,1:T(8,128)(2,1)} %bitcast.60), calls=%async_computation.6 | async-start | bytes 393216 | tf_op jit(solution)/shard_map/all_to_all | solution.py:111
  362.2 65.6 %all-reduce.11.cloned.1.call-start = ((), (), s32[]{:S(2)}) async-start(), calls=%async_computation.16 | async-start | bytes 3145728 | tf_op jit(solution)/shard_map/psum | solution.py:55
  386.1 97.8 %all-reduce.13.cloned.1.call-start = ((), (), s32[]{:S(2)}) async-start(), calls=%async_computation.17 | async-start | bytes 3145728 | tf_op jit(solution)/shard_map/psum | solution.py:55
  440.8 121.5 %reduce-scatter.6.cloned.1.call-start = ((), (), s32[]{:S(2)}) async-start(), calls=%async_computation.18 | async-start | bytes 1310720 | tf_op jit(solution)/shard_map/reduce_scatter | solution.py:129
  526.8 94.4 %copy-start.81 = (f32[768]{0:T(1024)}, f32[768]{0:T(1024)S(1)}, u32[]{:S(2)}) copy-start(f32[768]{0:T(1024)S(1)} %add_divide_fusion.5) | copy-start | bytes 9220
  534.4 67.9 %all-gather.7.cloned.1.call-start = ((), (), s32[]{:S(2)}) async-start(), calls=%async_computation.19 | async-start | bytes 1310720 | tf_op jit(solution)/shard_map/all_gather | solution.py:83
  564.0 8.5 collective-permute-start.1
  625.9 15.0 %all-to-all-start.6 = ((bf16[128,4,192]{0,2,1:T(8,128)(2,1)}), bf16[128,4,192]{0,2,1:T(8,128)(2,1)S(1)}, u32[]{:S(2)}, u32[]{:S(2)}) async-start(bf16[128,4,192]{0,2,1:T(8,128)(2,1)} %bitcast.84), calls=%async_computation.8 | async-start | bytes 393216 | tf_op jit(solution)/shard_map/all_to_all | solution.py:112
  640.9 8.6 %all-to-all-start.7 = ((bf16[128,4,192]{0,2,1:T(8,128)(2,1)}), bf16[128,4,192]{0,2,1:T(8,128)(2,1)S(1)}, u32[]{:S(2)}, u32[]{:S(2)}) async-start(bf16[128,4,192]{0,2,1:T(8,128)(2,1)} %bitcast.87), calls=%async_computation.9 | async-start | bytes 393216 | tf_op jit(solution)/shard_map/all_to_all | solution.py:113
  649.5 8.6 %all-to-all-start.8 = ((bf16[128,4,192]{0,2,1:T(8,128)(2,1)}), bf16[128,4,192]{0,2,1:T(8,128)(2,1)S(1)}, u32[]{:S(2)}, u32[]{:S(2)}) async-start(bf16[128,4,192]{0,2,1:T(8,128)(2,1)} %bitcast.90), calls=%async_computation.10 | async-start | bytes 393216 | tf_op jit(solution)/shard_map/all_to_all | solution.py:111
  652.9 63.6 %all-reduce.15.cloned.1.call-start = ((), (), s32[]{:S(2)}) async-start(), calls=%async_computation.20 | async-start | bytes 3145728 | tf_op jit(solution)/shard_map/psum | solution.py:55
  674.8 97.7 %all-reduce.17.cloned.1.call-start = ((), (), s32[]{:S(2)}) async-start(), calls=%async_computation.21 | async-start | bytes 3145728 | tf_op jit(solution)/shard_map/psum | solution.py:55
  729.5 122.8 %reduce-scatter.8.cloned.1.call-start = ((), (), s32[]{:S(2)}) async-start(), calls=%async_computation.22 | async-start | bytes 1310720 | tf_op jit(solution)/shard_map/reduce_scatter | solution.py:129
  730.1 53.7 %copy-start.77 = (f32[512]{0:T(512)S(1)}, f32[512]{0:T(512)}, u32[]{:S(2)}) copy-start(f32[512]{0:T(512)} %copy-done.75) | copy-start | bytes 6148
  730.1 53.7 %copy-start.87 = (f32[512]{0:T(512)S(1)}, f32[512]{0:T(512)}, u32[]{:S(2)}) copy-start(f32[512]{0:T(512)} %add_divide_fusion.10) | copy-start | bytes 6148
  822.5 29.7 %copy-start.40 = (bf16[128,1024]{1,0:T(8,128)(2,1)S(1)}, bf16[128,1024]{1,0:T(8,128)(2,1)}, u32[]{:S(2)}) copy-start(bf16[128,1024]{1,0:T(8,128)(2,1)} %bitcast_select_fusion) | copy-start | bytes 786436
  (93 other events, 588.8 us)
Sparse Core Ops, SparseCore 0:
  8.9 30.6 all-gather.8
  108.3 41.5 all-reduce.6
  158.9 42.9 all-reduce.8
  244.6 27.7 reduce-scatter.3
  284.5 27.8 all-gather.4
  386.2 41.5 all-reduce.10
  440.9 42.9 all-reduce.12
  534.5 27.7 reduce-scatter.5
  574.4 27.8 all-gather.6
  674.9 41.5 all-reduce.14
  729.6 42.8 all-reduce.16
  824.5 27.7 reduce-scatter.7
where the time goes:
time: 873 us; the launch traced here: 862 us
  waiting for transfers between devices  431 us (49%)
  blocking collectives  145 us (17%)
  matrix products  131 us (15%)
  other arithmetic  53 us (6%)
  local copies, waits for them, and re-layouts  42.2 us (5%)
  starting transfers between devices  37.5 us (4%)
  between operations  21.7 us (2%)
    psum x6, waiting for transfers between devices, orthogonal_updates(): grams = lax.psum(partial_grams.astype(jnp.bfloat16), 'seq')  249 us
    reduce_scatter x3, waiting for transfers between devices, run_section(): lax.psum_scatter(head_terms.astype(jnp.bfloat16), 'head', scatter_dimensi...  83.7 us
    all_gather x3, waiting for transfers between devices, run_section(): whole = lax.all_gather(residual, 'head', axis=1, tiled=True)  69.2 us
    dot_general x18, matrix products, orthogonal_updates(): jnp.dot(mixing, block, preferred_element_type=jnp.float32)  43.4 us
    unnamed x207, local copies, waits for them, and re-layouts  27 us
    all_gather x3, blocking collectives, orthogonal_updates(): lax.all_gather(current[1], 'seq', axis=1, tiled=True)  26.8 us
    dot_general x3, matrix products, run_section(): projected = jnp.dot(normed, qkv_matrix, preferred_element_type=jnp.float32)  26.8 us
    all_gather x3, blocking collectives, orthogonal_updates(): lax.all_gather(current[0], 'seq', axis=1, tiled=True)  26.6 us
  transfers between devices with their start and end apart: 23, of which 20 were waited for; matrix products, arithmetic and copies ran while one was open for 5% of the time, Pallas kernels for 0%

commit v1 on v0

v1 whole, which is shorter than its diff:
```python
import jax
import jax.numpy as jnp
from jax import lax
from jax.sharding import PartitionSpec as P

NS_STEPS = 2


ns_first = 3.4445
ns_second = -4.775
ns_third = 2.0315
update_step = 1.0
norm_eps = 1e-06
grad_eps = 1e-07


def shifted(array, axis, by):
    devices = lax.axis_size(axis)
    pairs = [(i, i + by) for i in range(devices) if 0 <= i + by < devices]
    return lax.ppermute(array, axis, pairs)


def rms_scale(values):
    return values * lax.rsqrt(jnp.mean(values * values, axis=-1, keepdims=True) + norm_eps)


def contract_rows(left, right):
    return lax.dot_general(
        left, right, (((0,), (0,)), ((), ())), preferred_element_type=jnp.float32
    )


def renormalize(weights, target_norms):
    return weights * (target_norms / (jnp.sqrt(jnp.sum(weights * weights, axis=0)) + norm_eps))


def dot(left, right):
    return jnp.dot(left, right, preferred_element_type=jnp.float32)


def orthogonalize(gradient):
    current = (gradient / (jnp.sqrt(jnp.sum(gradient * gradient)) + grad_eps)).astype(jnp.bfloat16)
    for sweep_index in range(NS_STEPS):
        gram_matrix = lax.dot_general(
            current, current, (((1,), (1,)), ((), ())), preferred_element_type=jnp.float32
        ).astype(jnp.bfloat16)
        square = dot(gram_matrix, gram_matrix)
        mixing = (ns_second * gram_matrix.astype(jnp.float32) + ns_third * square).astype(
            jnp.bfloat16
        )
        current = (ns_first * current.astype(jnp.float32) + dot(mixing, current)).astype(
            jnp.bfloat16
        )
    return current


def gather_heads(block):
    heads = lax.axis_size("head")
    spread = jnp.broadcast_to(block[None], (heads,) + block.shape)
    return lax.all_to_all(spread, "head", split_axis=0, concat_axis=0, tiled=True)


def run_section(
    residual, gain_row, qkv_matrix, head_gains, rate_row, out_gain_row, out_weights, fasts, norms
):
    values = residual.astype(jnp.float32)
    rows, width = residual.shape
    heads = lax.axis_size("head")
    head_width = head_gains.shape[-1]
    whole = gather_heads(residual).swapaxes(0, 1).reshape(rows, heads * width)
    normed = (rms_scale(whole.astype(jnp.float32)) * gain_row).astype(jnp.bfloat16)
    projected = dot(normed, qkv_matrix).reshape(rows, 3, head_width)
    queries = (rms_scale(projected[:, 0]) * head_gains[0]).astype(jnp.bfloat16)
    key_rows = (rms_scale(projected[:, 1]) * head_gains[1]).astype(jnp.bfloat16)
    out_grad = (-rate_row[:, None] * projected[:, 2]).astype(jnp.bfloat16)
    both = lax.all_gather(
        jnp.concatenate([key_rows, out_grad], axis=1), "seq", axis=0, tiled=True
    )
    keys, grads = both[:, :head_width], both[:, head_width:]
    gate_fast, up_fast, down_fast = fasts
    pre_gate = dot(keys, gate_fast.astype(jnp.bfloat16))
    pre_up = dot(keys, up_fast.astype(jnp.bfloat16))
    sigmoid_gate = jax.nn.sigmoid(pre_gate)
    gated = pre_gate * sigmoid_gate
    hidden = (gated * pre_up).astype(jnp.bfloat16)
    backward = lax.dot_general(
        grads,
        down_fast.astype(jnp.bfloat16),
        (((1,), (1,)), ((), ())),
        preferred_element_type=jnp.float32,
    )
    grad_gate = (backward * pre_up * sigmoid_gate * (1.0 + pre_gate * (1.0 - sigmoid_gate))).astype(
        jnp.bfloat16
    )
    grad_up = (backward * gated).astype(jnp.bfloat16)
    gate_step = orthogonalize(contract_rows(keys, grad_gate))
    up_step = orthogonalize(contract_rows(keys, grad_up))
    down_step = orthogonalize(contract_rows(grads, hidden))
    gate_fast = renormalize(gate_fast - update_step * gate_step.astype(jnp.float32), norms[0])
    up_fast = renormalize(up_fast - update_step * up_step.astype(jnp.float32), norms[1])
    down_fast = renormalize(down_fast - update_step * down_step.astype(jnp.float32).T, norms[2])
    gate_out = dot(queries, gate_fast.astype(jnp.bfloat16))
    up_out = dot(queries, up_fast.astype(jnp.bfloat16))
    output = dot(
        (jax.nn.silu(gate_out) * up_out).astype(jnp.bfloat16), down_fast.astype(jnp.bfloat16)
    )
    normed_out = (rms_scale(output) * out_gain_row).astype(jnp.bfloat16)
    head_terms = dot(normed_out, out_weights).astype(jnp.bfloat16)
    terms = head_terms.reshape(rows, heads, width).swapaxes(0, 1)
    parts = lax.all_to_all(terms, "head", split_axis=0, concat_axis=0, tiled=True)
    delta = jnp.sum(parts.astype(jnp.float32), axis=0)
    return ((values + delta).astype(jnp.bfloat16), (gate_fast, up_fast, down_fast))


def shards(stream, in_gain, w_qkv, qk_gain, w_one, w_three, w_two, token_rate, out_gain, w_out):
    segment_index = lax.axis_index("segment")
    span_count = stream.shape[0]
    moments = span_count + lax.axis_size("segment") - 1
    qkv_matrix = w_qkv[0].reshape(w_qkv.shape[1], -1)
    fasts = (
        w_one[0, 0].astype(jnp.float32),
        w_three[0, 0].astype(jnp.float32),
        w_two[0, 0].astype(jnp.float32),
    )
    norms = tuple((jnp.sqrt(jnp.sum(matrix * matrix, axis=0)) for matrix in fasts))
    received = jnp.zeros_like(stream[0])
    collected = jnp.zeros(stream.shape, jnp.bfloat16)
    for moment in range(moments):
        span_index = moment - segment_index
        active = (span_index >= 0) & (span_index < span_count)
        clipped = jnp.clip(span_index, 0, span_count - 1)
        source = jnp.where(segment_index == 0, stream[min(moment, span_count - 1)], received)
        rate_row = lax.dynamic_index_in_dim(token_rate[0], clipped, 0, keepdims=False)
        result, updated = run_section(
            source,
            in_gain[0],
            qkv_matrix,
            qk_gain[0, 0],
            rate_row,
            out_gain[0, 0],
            w_out[0, 0],
            fasts,
            norms,
        )
        fasts = tuple((jnp.where(active, fresh, former) for fresh, former in zip(updated, fasts)))
        chosen = jnp.arange(span_count) == span_index
        collected = jnp.where(chosen[:, None, None], result[None], collected)
        if moment + 1 < moments:
            received = shifted(result, "segment", 1)
    return collected[None]


def solution(mesh):
    placed = (
        P(None, "seq", "head"),
        P("segment", None),
        P("segment", None, "head", None, None),
        P("segment", "head", None, None),
        P("segment", "head", None, None),
        P("segment", "head", None, None),
        P("segment", "head", None, None),
        P("segment", None, "seq"),
        P("segment", "head", None),
        P("segment", "head", None, None),
    )
    return jax.shard_map(
        shards,
        mesh=mesh,
        in_specs=placed,
        out_specs=P("segment", None, "seq", "head"),
        check_vma=False,
    )
```

time: 873 us -> 509 us (0.58)
  waiting for transfers between devices: 431 us -> 89.2 us
  matrix products: 131 us -> 217 us
  other arithmetic: 53 us -> 13.2 us
  blocking collectives: 145 us -> 116 us
  starting transfers between devices: 37.5 us -> 18.3 us
  local copies, waits for them, and re-layouts: 42.2 us -> 28.2 us
    psum x6 -> x0, waiting for transfers between devices: 249 us -> none  [orthogonal_updates(): grams = lax.psum(partial_grams.astype(jnp.bfloat16), 'seq')]
    all_gather x15 -> x0, blocking collectives: 127 us -> none  [the longest x3 26.8 us: orthogonal_updates(): lax.all_gather(current[1], 'seq', axis=1, tiled=True)]
    all_to_all x0 -> x4, blocking collectives: none -> 116 us  [the longest x2 61.2 us: run_section(): lax.all_to_all(terms, 'head', split_axis=0, concat_axis=0, tiled=True)]
    reduce_scatter x3 -> x0, waiting for transfers between devices: 83.7 us -> none  [run_section(): lax.psum_scatter(head_terms.astype(jnp.bfloat16), 'head', scatter_dimensi...]
    dot_general x60 -> x57, matrix products: 111 us -> 184 us  [the longest x36 128 us: dot(): return jnp.dot(left, right, preferred_element_type=jnp.float32)]
    all_gather x3, waiting for transfers between devices: 69.2 us -> 47.1 us  [run_section(): lax.all_gather(jnp.concatenate([key_rows, out_grad], axis=1), 'seq', axis...]
    all_to_all x9 -> x2, starting transfers between devices: 30.3 us -> 11.1 us  [the longest x1 6.35 us: gather_heads(): lax.all_to_all(spread, 'head', split_axis=0, concat_axis=0, tiled=True)]
    psum x3 -> x0, blocking collectives: 17.9 us -> none  [orthogonal_updates(): totals = lax.psum(squares, 'seq')]
  transfers between devices with their start and end apart: 23 -> 7, of which waited for: 20 -> 7; matrix products, arithmetic and copies ran while one was open for 5% -> 4% of each run, Pallas kernels for 0% -> 0%
where the time goes in v1:
time: 509 us; the launch traced here: 503 us
  matrix products  217 us (43%)
  blocking collectives  116 us (23%)
  waiting for transfers between devices  89.2 us (18%)
  local copies, waits for them, and re-layouts  28.2 us (6%)
  between operations  21 us (4%)
  starting transfers between devices  18.3 us (4%)
  other arithmetic  13.2 us (3%)
    dot_general x36, matrix products, dot(): return jnp.dot(left, right, preferred_element_type=jnp.float32)  128 us
    all_to_all x2, blocking collectives, run_section(): lax.all_to_all(terms, 'head', split_axis=0, concat_axis=0, tiled=True)  61.2 us
    all_to_all x2, blocking collectives, gather_heads(): lax.all_to_all(spread, 'head', split_axis=0, concat_axis=0, tiled=True)  54.9 us
    dot_general x18, matrix products, orthogonalize(): lax.dot_general(current, current, (((1,), (1,)), ((), ())), preferred_ele...  49.1 us
    all_gather x3, waiting for transfers between devices, run_section(): lax.all_gather(jnp.concatenate([key_rows, out_grad], axis=1), 'seq', axis...  47.1 us
    dot_general x9, matrix products, contract_rows(): lax.dot_general(left, right, (((0,), (0,)), ((), ())), preferred_element_...  33.5 us
    all_to_all x1, waiting for transfers between devices, run_section(): lax.all_to_all(terms, 'head', split_axis=0, concat_axis=0, tiled=True)  26 us
    unnamed x139, local copies, waits for them, and re-layouts  22 us
  transfers between devices with their start and end apart: 7, of which 7 were waited for; matrix products, arithmetic and copies ran while one was open for 4% of the time, Pallas kernels for 0%

profile of v1, /device:TPU:0, one launch (start us, length us, event | category | flops | bytes accessed | tf_op | source)
XLA Modules:
  0.0 503.1 jit_solution(6374766848972372951)
XLA Ops:
  8.7 6.3 %all-to-all-start = ((bf16[4,128,1024]{2,1,0:T(8,128)(2,1)}), bf16[4,128,1024]{2,1,0:T(8,128)(2,1)S(1)}, u32[]{:S(2)}, u32[]{:S(2)}) async-start(bf16[4,128,1024]{2,1,0:T(8,128)(2,1)} %broadcast_in_dim.50), calls=%async_computation | async-start | bytes 2097152 | tf_op jit(solution)/shard_map/all_to_all | solution.py:60
  16.3 16.9 %copy.29 = bf16[1,4096,1,3,512]{1,4,3,2,0:T(8,128)(2,1)} copy(bf16[1,4096,1,3,512]{4,1,3,2,0:T(8,128)(2,1)} %param.12) | data formatting | bytes 25165824 | tf_op args[2]
  34.4 6.4 %all-to-all-done = bf16[4,128,1024]{2,1,0:T(8,128)(2,1)S(1)} async-done(((bf16[4,128,1024]{2,1,0:T(8,128)(2,1)}), bf16[4,128,1024]{2,1,0:T(8,128)(2,1)S(1)}, u32[]{:S(2)}, u32[]{:S(2)}) %all-to-all-start) | async-done | bytes 1048608 | tf_op jit(solution)/shard_map/all_to_all | solution.py:60
  42.7 8.9 %fusion.4 = f32[128,3,512]{2,0,1:T(8,128)S(1)} fusion(bf16[128,4096,1]{0,1,2:T(8,128)(2,1)S(1)} %bitcast.296, bf16[1,4096,1,3,512]{1,4,3,2,0:T(8,128)(2,1)} %copy.29), kind=kOutput, calls=%fused_computation.4 | convolution fusion | flops 1610612736 | bytes 14417920 | tf_op jit(solution)/shard_map/dot_general | solution.py:38
  53.7 15.4 %all-gather.4.cloned.1.call-done = bf16[512,1024]{1,0:T(8,128)(2,1)} async-done(((bf16[128,1024]{1,0:T(8,128)(2,1)}), bf16[512,1024]{1,0:T(8,128)(2,1)}) %all-gather.4.cloned.1.call-update) | async-done | bytes 1048592 | tf_op jit(solution)/shard_map/all_gather | solution.py:76
  76.6 4.8 multiply_reduce_fusion.17
  82.1 4.4 multiply_reduce_fusion.15
  103.0 4.2 add_convert_fusion.12
  110.0 4.1 fusion.19
  117.5 4.3 add_convert_fusion.2
  125.7 4.3 fusion.20
  137.4 30.6 %all_to_all.30 = bf16[4,128,1024]{2,1,0:T(8,128)(2,1)S(1)} all-to-all(bf16[4,128,1024]{2,1,0:T(8,128)(2,1)S(1)} %bitcast.298), channel_id=1, replica_groups=mesh['segment'=2,'seq'=4,'head'=4] {'head'}, dimensions={0} | all-to-all | bytes 2097152 | tf_op jit(solution)/shard_map/all_to_all | solution.py:110
  171.7 4.8 collective-permute-done
  176.7 27.4 %all_to_all.31 = bf16[4,128,1024]{2,1,0:T(8,128)(2,1)S(1)} all-to-all(bf16[4,128,1024]{2,1,0:T(8,128)(2,1)S(1)} %broadcast_in_dim.51), channel_id=1, replica_groups=mesh['segment'=2,'seq'=4,'head'=4] {'head'}, dimensions={0} | all-to-all | bytes 2097152 | tf_op jit(solution)/shard_map/all_to_all | solution.py:60
  206.0 8.9 %fusion.2 = f32[128,3,512]{2,0,1:T(8,128)S(1)} fusion(bf16[128,4096,1]{0,1,2:T(8,128)(2,1)S(1)} %bitcast.297, bf16[1,4096,1,3,512]{1,4,3,2,0:T(8,128)(2,1)} %copy.29), kind=kOutput, calls=%fused_computation.2 | convolution fusion | flops 1610612736 | bytes 14417920 | tf_op jit(solution)/shard_map/dot_general | solution.py:38
  216.3 15.7 %all-gather.6.cloned.1.call-done = bf16[512,1024]{1,0:T(8,128)(2,1)} async-done(((bf16[128,1024]{1,0:T(8,128)(2,1)}), bf16[512,1024]{1,0:T(8,128)(2,1)}) %all-gather.6.cloned.1.call-update) | async-done | bytes 1048592 | tf_op jit(solution)/shard_map/all_gather | solution.py:76
  240.6 4.8 multiply_reduce_fusion.11
  246.1 4.6 multiply_reduce_fusion.9
  273.0 4.3 multiply_reduce_fusion.8
  297.2 30.5 %all_to_all.32 = bf16[4,128,1024]{2,1,0:T(8,128)(2,1)S(1)} all-to-all(bf16[4,128,1024]{2,1,0:T(8,128)(2,1)S(1)} %bitcast.299), channel_id=1, replica_groups=mesh['segment'=2,'seq'=4,'head'=4] {'head'}, dimensions={0} | all-to-all | bytes 2097152 | tf_op jit(solution)/shard_map/all_to_all | solution.py:110
  331.4 4.8 collective-permute-done.1
  336.9 27.6 %all_to_all.33 = bf16[4,128,1024]{2,1,0:T(8,128)(2,1)} all-to-all(bf16[4,128,1024]{2,1,0:T(8,128)(2,1)S(1)} %broadcast_in_dim.52), channel_id=1, replica_groups=mesh['segment'=2,'seq'=4,'head'=4] {'head'}, dimensions={0} | all-to-all | bytes 2097152 | tf_op jit(solution)/shard_map/all_to_all | solution.py:60
  367.4 8.9 %fusion = f32[128,3,512]{2,0,1:T(8,128)S(1)} fusion(bf16[128,4096,1]{0,1,2:T(8,128)(2,1)S(1)} %bitcast.295, bf16[1,4096,1,3,512]{1,4,3,2,0:T(8,128)(2,1)} %copy.29), kind=kOutput, calls=%fused_computation | convolution fusion | flops 1610612736 | bytes 14417920 | tf_op jit(solution)/shard_map/dot_general | solution.py:38
  377.3 16.0 %all-gather.8.cloned.1.call-done = bf16[512,1024]{1,0:T(8,128)(2,1)} async-done(((bf16[128,1024]{1,0:T(8,128)(2,1)}), bf16[512,1024]{1,0:T(8,128)(2,1)}) %all-gather.8.cloned.1.call-update) | async-done | bytes 1048592 | tf_op jit(solution)/shard_map/all_gather | solution.py:76
  407.2 4.6 multiply_reduce_fusion.3
  415.8 4.2 add_convert_fusion.6
  422.9 5.0 multiply_reduce_fusion.4
  430.4 4.0 add_convert_fusion.4
  437.2 5.0 multiply_reduce_fusion.2
  451.4 4.7 multiply_reduce_fusion
  464.1 4.7 all-to-all-start.5
  469.0 26.0 %all-to-all-done.5 = bf16[4,128,1024]{2,1,0:T(8,128)(2,1)S(1)} async-done(((bf16[4,128,1024]{2,1,0:T(8,128)(2,1)}), bf16[4,128,1024]{2,1,0:T(8,128)(2,1)S(1)}, u32[]{:S(2)}, u32[]{:S(2)}) %all-to-all-start.5) | async-done | bytes 1048608 | tf_op jit(solution)/shard_map/all_to_all | solution.py:110
  (255 shorter events, 154.9 us)
Async XLA Ops:
  7.5 8.0 %copy-start.52 = (f32[1,4096]{1,0:T(1,128)S(1)}, f32[1,4096]{1,0:T(1,128)}, u32[]{:S(2)}) copy-start(f32[1,4096]{1,0:T(1,128)} %param.11) | copy-start | bytes 49156
  8.7 32.1 %all-to-all-start = ((bf16[4,128,1024]{2,1,0:T(8,128)(2,1)}), bf16[4,128,1024]{2,1,0:T(8,128)(2,1)S(1)}, u32[]{:S(2)}, u32[]{:S(2)}) async-start(bf16[4,128,1024]{2,1,0:T(8,128)(2,1)} %broadcast_in_dim.50), calls=%async_computation | async-start | bytes 2097152 | tf_op jit(solution)/shard_map/all_to_all | solution.py:60
  15.0 54.1 %all-gather.4.cloned.1.call-start = ((), (), s32[]{:S(2)}) async-start(), calls=%async_computation.6 | async-start | bytes 1310720 | tf_op jit(solution)/shard_map/all_gather | solution.py:76
  16.3 17.0 %copy-start.56 = (f32[1,2,128]{2,1,0:T(2,128)S(1)}, f32[1,2,128]{2,1,0:T(2,128)}, u32[]{:S(2)}) copy-start(f32[1,2,128]{2,1,0:T(2,128)} %param.17) | copy-start | bytes 3076
  16.3 17.5 %copy-start.55 = (f32[1,1,2,512]{3,2,1,0:T(2,128)S(1)}, f32[1,1,2,512]{3,2,1,0:T(2,128)}, u32[]{:S(2)}) copy-start(f32[1,1,2,512]{3,2,1,0:T(2,128)} %param.13) | copy-start | bytes 12292
  34.4 17.9 %copy-start.46 = (f32[1,1,1,512]{3,2,1,0:T(1,128)}, f32[1,1,1,512]{3,2,1,0:T(1,128)S(1)}, u32[]{:S(2)}) copy-start(f32[1,1,1,512]{3,2,1,0:T(1,128)S(1)} %get-tuple-element.24) | copy-start | bytes 6148
  52.3 16.8 %copy-start = (bf16[1,1,512,768]{3,2,1,0:T(8,128)(2,1)S(1)}, bf16[1,1,512,768]{3,2,1,0:T(8,128)(2,1)}, u32[]{:S(2)}) copy-start(bf16[1,1,512,768]{3,2,1,0:T(8,128)(2,1)} %param.14) | copy-start | bytes 2359300
  53.2 178.8 %all-gather.6.cloned.1.call-start = ((), (), s32[]{:S(2)}) async-start(), calls=%async_computation.7 | async-start | bytes 1310720 | tf_op jit(solution)/shard_map/all_gather | solution.py:76
  53.7 78.1 %copy-start.7 = (bf16[1,1,768,512]{2,3,1,0:T(8,128)(2,1)}, bf16[1,1,768,512]{2,3,1,0:T(8,128)(2,1)S(1)}, u32[]{:S(2)}) copy-start(bf16[1,1,768,512]{2,3,1,0:T(8,128)(2,1)S(1)} %copy.31) | copy-start | bytes 2359300
  76.6 5.5 %copy-start.24 = (bf16[512,1024]{1,0:T(8,128)(2,1)S(1)}, bf16[512,1024]{1,0:T(8,128)(2,1)}, u32[]{:S(2)}) copy-start(bf16[512,1024]{1,0:T(8,128)(2,1)} %all-gather.4.cloned.1.call-done) | copy-start | bytes 3145732
  99.4 25.1 %copy-start.43 = (f32[768]{0:T(1024)}, f32[768]{0:T(1024)S(1)}, u32[]{:S(2)}) copy-start(f32[768]{0:T(1024)S(1)} %get-tuple-element.11) | copy-start | bytes 9220
  99.4 31.3 %copy-start.11 = (bf16[512,768]{1,0:T(8,128)(2,1)}, bf16[512,768]{1,0:T(8,128)(2,1)S(1)}, u32[]{:S(2)}) copy-start(bf16[512,768]{1,0:T(8,128)(2,1)S(1)} %get-tuple-element.36) | copy-start | bytes 2359300
  114.2 11.0 %copy-start.41 = (f32[768]{0:T(1024)}, f32[768]{0:T(1024)S(1)}, u32[]{:S(2)}) copy-start(f32[768]{0:T(1024)S(1)} %get-tuple-element.13) | copy-start | bytes 9220
  137.4 30.8 %copy-start.4 = (bf16[2,128,1024]{2,1,0:T(8,128)(2,1)S(1)}, bf16[2,128,1024]{2,1,0:T(8,128)(2,1)}, u32[]{:S(2)}) copy-start(bf16[2,128,1024]{2,1,0:T(8,128)(2,1)} %param.10) | copy-start | bytes 1572868
  168.2 8.5 %copy-start.2 = (f32[128,1024]{1,0:T(8,128)}, f32[128,1024]{1,0:T(8,128)S(1)}, u32[]{:S(2)}) copy-start(f32[128,1024]{1,0:T(8,128)S(1)} %convert_reduce_fusion.2) | copy-start | bytes 1572868
  168.3 8.2 %collective-permute-start = (bf16[128,1024]{1,0:T(8,128)(2,1)S(1)}, bf16[128,1024]{1,0:T(8,128)(2,1)S(1)}, u32[]{:S(2)}, u32[]{:S(2)}) collective-permute-start(bf16[128,1024]{1,0:T(8,128)(2,1)S(1)} %add_convert_fusion.17), channel_id=1, source_target_pairs={{0,16},{1,17},{2,18},{3,19},{4,20},{5,21},{6,22},{7,23},{8,24},{9,... | collective-permute-start | bytes 786440 | tf_op jit(solution)/shard_map/ppermute | solution.py:20
  206.0 9.1 %copy-start.47 = (f32[1,1,1,512]{3,2,1,0:T(1,128)S(1)}, f32[1,1,1,512]{3,2,1,0:T(1,128)}, u32[]{:S(2)}) copy-start(f32[1,1,1,512]{3,2,1,0:T(1,128)} %copy-done.46) | copy-start | bytes 6148
  206.0 9.1 %copy-start.58 = (f32[128]{0:T(128)S(1)}, f32[128]{0:T(128)}, u32[]{:S(2)}) copy-start(f32[128]{0:T(128)} %get-tuple-element.27) | copy-start | bytes 1540
  215.0 17.0 %copy-start.12 = (bf16[512,768]{1,0:T(8,128)(2,1)S(1)}, bf16[512,768]{1,0:T(8,128)(2,1)}, u32[]{:S(2)}) copy-start(bf16[512,768]{1,0:T(8,128)(2,1)} %copy-done.11) | copy-start | bytes 2359300
  215.0 17.0 %copy-start.45 = (f32[768]{0:T(1024)S(1)}, f32[768]{0:T(1024)}, u32[]{:S(2)}) copy-start(f32[768]{0:T(1024)} %add_divide_fusion.8) | copy-start | bytes 9220
  216.0 177.3 %all-gather.8.cloned.1.call-start = ((), (), s32[]{:S(2)}) async-start(), calls=%async_computation.8 | async-start | bytes 1310720 | tf_op jit(solution)/shard_map/all_gather | solution.py:76
  216.3 17.6 %copy-start.14 = (bf16[1,1,512,768]{3,2,1,0:T(8,128)(2,1)S(1)}, bf16[1,1,512,768]{3,2,1,0:T(8,128)(2,1)}, u32[]{:S(2)}) copy-start(bf16[1,1,512,768]{3,2,1,0:T(8,128)(2,1)} %param.15) | copy-start | bytes 2359300
  216.3 17.6 %copy-start.53 = (f32[768]{0:T(1024)S(1)}, f32[768]{0:T(1024)}, u32[]{:S(2)}) copy-start(f32[768]{0:T(1024)} %add_divide_fusion.7) | copy-start | bytes 9220
  240.6 4.8 copy-start.64
  327.7 8.5 %copy-start.5 = (bf16[2,128,1024]{2,1,0:T(8,128)(2,1)S(1)}, bf16[2,128,1024]{2,1,0:T(8,128)(2,1)}, u32[]{:S(2)}) copy-start(bf16[2,128,1024]{2,1,0:T(8,128)(2,1)} %param.10) | copy-start | bytes 1572868
  328.0 8.4 %copy-start.35 = (bf16[128,1024]{1,0:T(8,128)(2,1)}, bf16[128,1024]{1,0:T(8,128)(2,1)S(1)}, u32[]{:S(2)}) copy-start(bf16[128,1024]{1,0:T(8,128)(2,1)S(1)} %add_convert_fusion.16) | copy-start | bytes 786436
  328.0 8.2 %collective-permute-start.1 = (bf16[128,1024]{1,0:T(8,128)(2,1)S(1)}, bf16[128,1024]{1,0:T(8,128)(2,1)S(1)}, u32[]{:S(2)}, u32[]{:S(2)}) collective-permute-start(bf16[128,1024]{1,0:T(8,128)(2,1)S(1)} %add_convert_fusion.16), channel_id=1, source_target_pairs={{0,16},{1,17},{2,18},{3,19},{4,20},{5,21},{6,22},{7,23},{8,24},{9,... | collective-permute-start | bytes 786440 | tf_op jit(solution)/shard_map/ppermute | solution.py:20
  367.4 9.1 %copy-start.57 = (f32[128]{0:T(128)S(1)}, f32[128]{0:T(128)}, u32[]{:S(2)}) copy-start(f32[128]{0:T(128)} %get-tuple-element.25) | copy-start | bytes 1540
  464.1 4.8 copy-start.6
  464.1 30.8 %all-to-all-start.5 = ((bf16[4,128,1024]{2,1,0:T(8,128)(2,1)}), bf16[4,128,1024]{2,1,0:T(8,128)(2,1)S(1)}, u32[]{:S(2)}, u32[]{:S(2)}) async-start(bf16[4,128,1024]{2,1,0:T(8,128)(2,1)} %bitcast.290), calls=%async_computation.5 | async-start | bytes 2097152 | tf_op jit(solution)/shard_map/all_to_all | solution.py:110
  468.8 26.3 %copy-start.21 = (bf16[128,1024]{1,0:T(8,128)(2,1)S(1)}, bf16[128,1024]{1,0:T(8,128)(2,1)}, u32[]{:S(2)}) copy-start(bf16[128,1024]{1,0:T(8,128)(2,1)} %copy-done.20) | copy-start | bytes 786436
  468.9 26.3 %copy-start.36 = (bf16[128,1024]{1,0:T(8,128)(2,1)S(1)}, bf16[128,1024]{1,0:T(8,128)(2,1)}, u32[]{:S(2)}) copy-start(bf16[128,1024]{1,0:T(8,128)(2,1)} %copy-done.35) | copy-start | bytes 786436
  (43 other events, 109.1 us)
Sparse Core Ops, SparseCore 0:
  53.3 15.7 all-gather.3
  216.1 15.8 all-gather.5
  377.4 15.8 all-gather.7

commit v2 on v1

v2 whole, which is shorter than its diff:
```python
import jax
import jax.numpy as jnp
from jax import lax
from jax.experimental import pallas as pl
from jax.experimental.pallas import tpu as pltpu
from jax.sharding import PartitionSpec as P

NS_STEPS = 2


ns_first = 3.4445
ns_second = -4.775
ns_third = 2.0315
update_step = 1.0
norm_eps = 1e-06
grad_eps = 1e-07


def shifted(array, axis, by):
    devices = lax.axis_size(axis)
    pairs = [(i, i + by) for i in range(devices) if 0 <= i + by < devices]
    return lax.ppermute(array, axis, pairs)


def rms_scale(values):
    return values * lax.rsqrt(jnp.mean(values * values, axis=-1, keepdims=True) + norm_eps)


def dot(left, right):
    return jnp.dot(left, right, preferred_element_type=jnp.float32)


def contract(left, right, dims):
    return lax.dot_general(
        left, right, ((dims[:1], dims[1:]), ((), ())), preferred_element_type=jnp.float32
    )


def fast_kernel(
    active_ref,
    both_ref,
    query_ref,
    gate_ref,
    up_ref,
    down_ref,
    wide_norms_ref,
    down_norm_ref,
    out_gain_ref,
    out_weights_hbm,
    terms_ref,
    new_gate_ref,
    new_up_ref,
    new_down_ref,
    rights,
    work,
    out_weights,
    out_sem,
):
    fetch = pltpu.make_async_copy(out_weights_hbm, out_weights, out_sem)
    fetch.start()
    tokens = both_ref.shape[1]
    rows = query_ref.shape[0]
    chunk = 2 * rows if tokens % (2 * rows) == 0 else rows
    work[0] = gate_ref[...].astype(jnp.bfloat16)
    work[1] = up_ref[...].astype(jnp.bfloat16)
    work[2] = down_ref[...].astype(jnp.bfloat16)

    def gradients(index, carry):
        here = pl.ds(pl.multiple_of(index * chunk, chunk), chunk)
        keys = both_ref[0, here, :]
        grads = both_ref[1, here, :]
        pre_gate = dot(keys, work[0])
        pre_up = dot(keys, work[1])
        backward = dot(grads, work[2])
        sigmoid_gate = jax.nn.sigmoid(pre_gate)
        gated = pre_gate * sigmoid_gate
        rights[0, here, :] = (
            backward * pre_up * sigmoid_gate * (1.0 + pre_gate * (1.0 - sigmoid_gate))
        ).astype(jnp.bfloat16)
        rights[1, here, :] = (backward * gated).astype(jnp.bfloat16)
        rights[2, here, :] = (gated * pre_up).astype(jnp.bfloat16)
        return carry

    lax.fori_loop(0, tokens // chunk, gradients, 0)

    def orthogonalize(index, carry):
        gradient = contract(both_ref[index // 2], rights[index], (0, 0))
        scale = 1.0 / (jnp.sqrt(jnp.sum(gradient * gradient, keepdims=True)) + grad_eps)
        work[index] = (gradient * scale).astype(jnp.bfloat16)

        def sweep(step, inner):
            current = work[index]
            gram_matrix = contract(current, current, (1, 1)).astype(jnp.bfloat16)
            square = dot(gram_matrix, gram_matrix)
            mixing = (ns_second * gram_matrix.astype(jnp.float32) + ns_third * square).astype(
                jnp.bfloat16
            )
            work[index] = (ns_first * current.astype(jnp.float32) + dot(mixing, current)).astype(
                jnp.bfloat16
            )
            return inner

        return lax.fori_loop(0, NS_STEPS, sweep, carry)

    lax.fori_loop(0, 3, orthogonalize, 0)

    active = active_ref[0] > 0
    for index, old_ref, new_ref, axis, target in (
        (0, gate_ref, new_gate_ref, 0, wide_norms_ref[0]),
        (1, up_ref, new_up_ref, 0, wide_norms_ref[1]),
        (2, down_ref, new_down_ref, 1, down_norm_ref[...]),
    ):
        moved = old_ref[...] - update_step * work[index].astype(jnp.float32)
        length = jnp.sqrt(jnp.sum(moved * moved, axis=axis, keepdims=True)) + norm_eps
        fresh = moved * (target / length)
        work[index] = fresh.astype(jnp.bfloat16)
        new_ref[...] = jnp.where(active, fresh, old_ref[...])

    gate_out = dot(query_ref[...], work[0])
    up_out = dot(query_ref[...], work[1])
    inner = (gate_out * jax.nn.sigmoid(gate_out) * up_out).astype(jnp.bfloat16)
    output = contract(inner, work[2], (1, 1))
    normed_out = (rms_scale(output) * out_gain_ref[...]).astype(jnp.bfloat16)
    fetch.wait()
    width = terms_ref.shape[2]

    def project(index, carry):
        columns = pl.ds(pl.multiple_of(index * width, width), width)
        terms_ref[index] = dot(normed_out, out_weights[:, columns]).astype(jnp.bfloat16)
        return carry

    lax.fori_loop(0, terms_ref.shape[0], project, 0)


def fast_step(active, both, queries, fasts, norms, out_gain_row, out_weights, heads):
    rows = queries.shape[0]
    inner, wide = fasts[0].shape
    width = out_weights.shape[1] // heads
    vmem = pl.BlockSpec(memory_space=pltpu.VMEM)
    state = jax.ShapeDtypeStruct((inner, wide), jnp.float32)
    return pl.pallas_call(
        fast_kernel,
        name="fast_step",
        out_shape=(jax.ShapeDtypeStruct((heads, rows, width), jnp.bfloat16), state, state, state),
        in_specs=[pl.BlockSpec(memory_space=pltpu.SMEM)]
        + [vmem] * 8
        + [pl.BlockSpec(memory_space=pl.ANY)],
        out_specs=(vmem,) * 4,
        scratch_shapes=[
            pltpu.VMEM((3, both.shape[1], wide), jnp.bfloat16),
            pltpu.VMEM((3, inner, wide), jnp.bfloat16),
            pltpu.VMEM(out_weights.shape, jnp.bfloat16),
            pltpu.SemaphoreType.DMA,
        ],
        compiler_params=pltpu.CompilerParams(vmem_limit_bytes=60 * 1024 * 1024),
        cost_estimate=pl.CostEstimate(
            flops=10**10, bytes_accessed=2 * 10**7, transcendentals=0
        ),
    )(active, both, queries, *fasts, *norms, out_gain_row, out_weights)


def gather_heads(block):
    heads = lax.axis_size("head")
    spread = jnp.broadcast_to(block[None], (heads,) + block.shape)
    return lax.all_to_all(spread, "head", split_axis=0, concat_axis=0, tiled=True)


def run_section(
    residual, gain_row, qkv_matrix, head_gains, rate_row, out_gain_row, out_weights, fasts, norms, active
):
    values = residual.astype(jnp.float32)
    rows, width = residual.shape
    heads = lax.axis_size("head")
    head_width = head_gains.shape[-1]
    whole = gather_heads(residual).swapaxes(0, 1).reshape(rows, heads * width)
    normed = (rms_scale(whole.astype(jnp.float32)) * gain_row).astype(jnp.bfloat16)
    projected = dot(normed, qkv_matrix).reshape(rows, 3, head_width)
    queries = (rms_scale(projected[:, 0]) * head_gains[0]).astype(jnp.bfloat16)
    key_rows = (rms_scale(projected[:, 1]) * head_gains[1]).astype(jnp.bfloat16)
    out_grad = (-rate_row[:, None] * projected[:, 2]).astype(jnp.bfloat16)
    both = lax.all_gather(jnp.stack([key_rows, out_grad]), "seq", axis=1, tiled=True)
    terms, *fasts = fast_step(
        active, both, queries, fasts, norms, out_gain_row, out_weights, heads
    )
    parts = lax.all_to_all(terms, "head", split_axis=0, concat_axis=0, tiled=True)
    delta = jnp.sum(parts.astype(jnp.float32), axis=0)
    return ((values + delta).astype(jnp.bfloat16), tuple(fasts))


def shards(stream, in_gain, w_qkv, qk_gain, w_one, w_three, w_two, token_rate, out_gain, w_out):
    segment_index = lax.axis_index("segment")
    span_count = stream.shape[0]
    moments = span_count + lax.axis_size("segment") - 1
    qkv_matrix = w_qkv[0].reshape(w_qkv.shape[1], -1)
    fasts = (
        w_one[0, 0].astype(jnp.float32),
        w_three[0, 0].astype(jnp.float32),
        w_two[0, 0].astype(jnp.float32).T,
    )
    norms = (
        jnp.stack([jnp.sqrt(jnp.sum(matrix * matrix, axis=0, keepdims=True)) for matrix in fasts[:2]]),
        jnp.sqrt(jnp.sum(fasts[2] * fasts[2], axis=1, keepdims=True)),
    )
    received = jnp.zeros_like(stream[0])
    collected = jnp.zeros(stream.shape, jnp.bfloat16)
    for moment in range(moments):
        span_index = moment - segment_index
        active = (span_index >= 0) & (span_index < span_count)
        clipped = jnp.clip(span_index, 0, span_count - 1)
        source = jnp.where(segment_index == 0, stream[min(moment, span_count - 1)], received)
        rate_row = lax.dynamic_index_in_dim(token_rate[0], clipped, 0, keepdims=False)
        result, fasts = run_section(
            source,
            in_gain[0],
            qkv_matrix,
            qk_gain[0, 0],
            rate_row,
            out_gain[0, :1],
            w_out[0, 0],
            fasts,
            norms,
            active.astype(jnp.int32)[None],
        )
        chosen = jnp.arange(span_count) == span_index
        collected = jnp.where(chosen[:, None, None], result[None], collected)
        if moment + 1 < moments:
            received = shifted(result, "segment", 1)
    return collected[None]


def solution(mesh):
    placed = (
        P(None, "seq", "head"),
        P("segment", None),
        P("segment", None, "head", None, None),
        P("segment", "head", None, None),
        P("segment", "head", None, None),
        P("segment", "head", None, None),
        P("segment", "head", None, None),
        P("segment", None, "seq"),
        P("segment", "head", None),
        P("segment", "head", None, None),
    )
    return jax.shard_map(
        shards,
        mesh=mesh,
        in_specs=placed,
        out_specs=P("segment", None, "seq", "head"),
        check_vma=False,
    )
```

time: 509 us -> 366 us (0.72); the launches traced: 503 us -> 365 us
  matrix products: 217 us -> 26.8 us
  Pallas kernels: 0 us -> 68.8 us
  between operations: 21 us -> 13.5 us
  waiting for transfers between devices: 89.2 us -> 83 us
  local copies, waits for them, and re-layouts: 28.2 us -> 22.1 us
    dot_general x36 -> x3, matrix products: 128 us -> 26.8 us  [dot(): return jnp.dot(left, right, preferred_element_type=jnp.float32)]
    dot_general x30 -> x0, matrix products: 89.1 us -> none  [the longest x18 49.1 us: orthogonalize(): lax.dot_general(current, current, (((1,), (1,)), ((), ())), preferred_ele...]
    pallas_call x0 -> x3, Pallas kernels: none -> 68.8 us  [fast_step(): pl.pallas_call(fast_kernel, name='fast_step', out_shape=(jax.ShapeDtypeSt...]
    all_gather x3, waiting for transfers between devices: 47.1 us -> 40.5 us  [run_section(): lax.all_gather(jnp.stack([key_rows, out_grad]), 'seq', axis=1, tiled=True)]
    unnamed x139 -> x28, local copies, waits for them, and re-layouts: 22 us -> 17.8 us
  transfers between devices with their start and end apart: 7 -> 7, of which waited for: 7 -> 7; matrix products, arithmetic and copies ran while one was open for 4% -> 7% of each run, Pallas kernels for 0% -> 0%
where the time goes in v2:
time: 366 us; the launch traced here: 365 us
  blocking collectives  116 us (32%)
  waiting for transfers between devices  83 us (23%)
  Pallas kernels  68.8 us (19%)
  matrix products  26.8 us (7%)
  local copies, waits for them, and re-layouts  22.1 us (6%)
  starting transfers between devices  18.3 us (5%)
  other arithmetic  16.6 us (5%)
  between operations  13.5 us (4%)
    pallas_call x3, Pallas kernels, fast_step(): pl.pallas_call(fast_kernel, name='fast_step', out_shape=(jax.ShapeDtypeSt...  68.8 us
    all_to_all x2, blocking collectives, run_section(): lax.all_to_all(terms, 'head', split_axis=0, concat_axis=0, tiled=True)  61.6 us
    all_to_all x2, blocking collectives, gather_heads(): lax.all_to_all(spread, 'head', split_axis=0, concat_axis=0, tiled=True)  54.8 us
    all_gather x3, waiting for transfers between devices, run_section(): lax.all_gather(jnp.stack([key_rows, out_grad]), 'seq', axis=1, tiled=True)  40.5 us
    dot_general x3, matrix products, dot(): return jnp.dot(left, right, preferred_element_type=jnp.float32)  26.8 us
    all_to_all x1, waiting for transfers between devices, run_section(): lax.all_to_all(terms, 'head', split_axis=0, concat_axis=0, tiled=True)  26 us
    unnamed x28, local copies, waits for them, and re-layouts  17.8 us
    ppermute x2, waiting for transfers between devices, shifted(): return lax.ppermute(array, axis, pairs)  9.63 us
  transfers between devices with their start and end apart: 7, of which 7 were waited for; matrix products, arithmetic and copies ran while one was open for 7% of the time, Pallas kernels for 0%

profile of v2, /device:TPU:0, one launch (start us, length us, event | category | flops | bytes accessed | tf_op | source)
XLA Modules:
  0.0 365.5 jit_solution(3994276641643837862)
XLA Ops:
  6.5 1.0 fusion.29
  7.6 1.2 broadcast_in_dim.103
  8.8 6.5 %all-to-all-start = ((bf16[4,128,1024]{2,1,0:T(8,128)(2,1)}), bf16[4,128,1024]{2,1,0:T(8,128)(2,1)S(1)}, u32[]{:S(2)}, u32[]{:S(2)}) async-start(bf16[4,128,1024]{2,1,0:T(8,128)(2,1)} %broadcast_in_dim.103), calls=%async_computation | async-start | bytes 2097152 | tf_op jit(solution)/shard_map/all_to_all | solution.py:165
  17.2 16.9 %copy.23 = bf16[1,4096,1,3,512]{1,4,3,2,0:T(8,128)(2,1)} copy(bf16[1,4096,1,3,512]{4,1,3,2,0:T(8,128)(2,1)} %param.12) | data formatting | bytes 25165824 | tf_op args[2]
  34.2 6.8 %all-to-all-done = bf16[4,128,1024]{2,1,0:T(8,128)(2,1)S(1)} async-done(((bf16[4,128,1024]{2,1,0:T(8,128)(2,1)}), bf16[4,128,1024]{2,1,0:T(8,128)(2,1)S(1)}, u32[]{:S(2)}, u32[]{:S(2)}) %all-to-all-start) | async-done | bytes 1048608 | tf_op jit(solution)/shard_map/all_to_all | solution.py:165
  42.9 8.9 %fusion.4 = f32[128,3,512]{2,0,1:T(8,128)S(1)} fusion(bf16[128,4096,1]{0,1,2:T(8,128)(2,1)S(1)} %bitcast.132, bf16[1,4096,1,3,512]{1,4,3,2,0:T(8,128)(2,1)} %copy.23), kind=kOutput, calls=%fused_computation.4 | convolution fusion | flops 1610612736 | bytes 14417920 | tf_op jit(solution)/shard_map/dot_general | solution.py:30
  52.1 0.7 pad_maximum_fusion
  53.3 0.9 copy.26.down_norm_ref
  54.2 1.3 convert_bitcast_fusion.down_ref
  55.5 1.9 bitcast_convert_fusion
  57.5 0.8 multiply_convert_fusion.2.query_ref
  58.3 10.6 %all-gather.4.cloned.1.call-done.both_ref = bf16[2,512,512]{2,1,0:T(8,128)(2,1)} async-done(((bf16[2,128,512]{2,1,0:T(8,128)(2,1)}), bf16[2,512,512]{2,1,0:T(8,128)(2,1)}) %all-gather.4.cloned.1.call-update) | async-done | bytes 1048592 | tf_op jit(solution)/shard_map/all_gather | solution.py:181
  68.8 22.9 %fast_step.3 = (bf16[4,128,1024]{2,1,0:T(8,128)(2,1)}, f32[512,768]{1,0:T(8,128)}, f32[512,768]{1,0:T(8,128)}, f32[512,768]{1,0:T(8,128)}) custom-call(s32[1]{0:T(128)} %bitcast.2.active_ref, bf16[2,512,512]{2,1,0:T(8,128)(2,1)} %all-gather.4.cloned.1.call-done.both_ref, bf16[128,512]{1,0:T(8,128)(2,1)} %multiply_convert_fusion.2.query_ref, ...), custom_call_target="tpu_custom_call" | custom-call | flops 10000000000 | bytes 20000000 | tf_op jit(solution)/shard_map/fast_step/pallas_call | solution.py:141
  91.8 30.9 %all_to_all.30 = bf16[4,128,1024]{2,1,0:T(8,128)(2,1)S(1)} all-to-all(bf16[4,128,1024]{2,1,0:T(8,128)(2,1)} %get-tuple-element.14), channel_id=1, replica_groups=mesh['segment'=2,'seq'=4,'head'=4] {'head'}, dimensions={0} | all-to-all | bytes 2097152 | tf_op jit(solution)/shard_map/all_to_all | solution.py:185
  122.9 3.4 collective-permute-start
  126.3 4.8 %collective-permute-done = bf16[128,1024]{1,0:T(8,128)(2,1)S(1)} collective-permute-done((bf16[128,1024]{1,0:T(8,128)(2,1)S(1)}, bf16[128,1024]{1,0:T(8,128)(2,1)S(1)}, u32[]{:S(2)}, u32[]{:S(2)}) %collective-permute-start) | collective-permute-done | bytes 262176 | tf_op jit(solution)/shard_map/ppermute | solution.py:22
  131.3 27.4 %all_to_all.31 = bf16[4,128,1024]{2,1,0:T(8,128)(2,1)S(1)} all-to-all(bf16[4,128,1024]{2,1,0:T(8,128)(2,1)S(1)} %broadcast_in_dim.106), channel_id=1, replica_groups=mesh['segment'=2,'seq'=4,'head'=4] {'head'}, dimensions={0} | all-to-all | bytes 2097152 | tf_op jit(solution)/shard_map/all_to_all | solution.py:165
  160.6 8.9 %fusion.2 = f32[128,3,512]{2,0,1:T(8,128)S(1)} fusion(bf16[128,4096,1]{0,1,2:T(8,128)(2,1)S(1)} %bitcast.133, bf16[1,4096,1,3,512]{1,4,3,2,0:T(8,128)(2,1)} %copy.23), kind=kOutput, calls=%fused_computation.2 | convolution fusion | flops 1610612736 | bytes 14417920 | tf_op jit(solution)/shard_map/dot_general | solution.py:30
  170.9 0.8 multiply_convert_fusion.1.query_ref
  171.7 14.9 %all-gather.6.cloned.1.call-done.both_ref = bf16[2,512,512]{2,1,0:T(8,128)(2,1)} async-done(((bf16[2,128,512]{2,1,0:T(8,128)(2,1)}), bf16[2,512,512]{2,1,0:T(8,128)(2,1)}) %all-gather.6.cloned.1.call-update) | async-done | bytes 1048592 | tf_op jit(solution)/shard_map/all_gather | solution.py:181
  186.5 22.9 %fast_step.4 = (bf16[4,128,1024]{2,1,0:T(8,128)(2,1)}, f32[512,768]{1,0:T(8,128)}, f32[512,768]{1,0:T(8,128)}, f32[512,768]{1,0:T(8,128)}) custom-call(s32[1]{0:T(128)} %bitcast.25.active_ref, bf16[2,512,512]{2,1,0:T(8,128)(2,1)} %all-gather.6.cloned.1.call-done.both_ref, bf16[128,512]{1,0:T(8,128)(2,1)} %multiply_convert_fusion.1.query_ref, ...), custom_call_target="tpu_custom_call" | custom-call | flops 10000000000 | bytes 20000000 | tf_op jit(solution)/shard_map/fast_step/pallas_call | solution.py:141
  209.5 30.7 %all_to_all.32 = bf16[4,128,1024]{2,1,0:T(8,128)(2,1)S(1)} all-to-all(bf16[4,128,1024]{2,1,0:T(8,128)(2,1)} %get-tuple-element.18), channel_id=1, replica_groups=mesh['segment'=2,'seq'=4,'head'=4] {'head'}, dimensions={0} | all-to-all | bytes 2097152 | tf_op jit(solution)/shard_map/all_to_all | solution.py:185
  240.5 3.4 collective-permute-start.1
  243.9 4.8 %collective-permute-done.1 = bf16[128,1024]{1,0:T(8,128)(2,1)S(1)} collective-permute-done((bf16[128,1024]{1,0:T(8,128)(2,1)S(1)}, bf16[128,1024]{1,0:T(8,128)(2,1)S(1)}, u32[]{:S(2)}, u32[]{:S(2)}) %collective-permute-start.1) | collective-permute-done | bytes 262176 | tf_op jit(solution)/shard_map/ppermute | solution.py:22
  248.8 27.4 %all_to_all.33 = bf16[4,128,1024]{2,1,0:T(8,128)(2,1)S(1)} all-to-all(bf16[4,128,1024]{2,1,0:T(8,128)(2,1)S(1)} %broadcast_in_dim.109), channel_id=1, replica_groups=mesh['segment'=2,'seq'=4,'head'=4] {'head'}, dimensions={0} | all-to-all | bytes 2097152 | tf_op jit(solution)/shard_map/all_to_all | solution.py:165
  278.2 8.9 %fusion = f32[128,3,512]{2,0,1:T(8,128)S(1)} fusion(bf16[128,4096,1]{0,1,2:T(8,128)(2,1)S(1)} %bitcast.131, bf16[1,4096,1,3,512]{1,4,3,2,0:T(8,128)(2,1)} %copy.23), kind=kOutput, calls=%fused_computation | convolution fusion | flops 1610612736 | bytes 14417920 | tf_op jit(solution)/shard_map/dot_general | solution.py:30
  288.2 0.7 multiply_convert_fusion.query_ref
  289.0 15.1 %all-gather.8.cloned.1.call-done.both_ref = bf16[2,512,512]{2,1,0:T(8,128)(2,1)} async-done(((bf16[2,128,512]{2,1,0:T(8,128)(2,1)}), bf16[2,512,512]{2,1,0:T(8,128)(2,1)}) %all-gather.8.cloned.1.call-update) | async-done | bytes 1048592 | tf_op jit(solution)/shard_map/all_gather | solution.py:181
  304.1 22.9 %fast_step.5 = (bf16[4,128,1024]{2,1,0:T(8,128)(2,1)}, f32[512,768]{1,0:T(8,128)}, f32[512,768]{1,0:T(8,128)}, f32[512,768]{1,0:T(8,128)}) custom-call(s32[1]{0:T(128)} %bitcast.35.active_ref, bf16[2,512,512]{2,1,0:T(8,128)(2,1)} %all-gather.8.cloned.1.call-done.both_ref, bf16[128,512]{1,0:T(8,128)(2,1)} %multiply_convert_fusion.query_ref, ...), custom_call_target="tpu_custom_call" | custom-call | flops 10000000000 | bytes 20000000 | tf_op jit(solution)/shard_map/fast_step/pallas_call | solution.py:141
  327.0 4.6 %all-to-all-start.5 = ((bf16[4,128,1024]{2,1,0:T(8,128)(2,1)}), bf16[4,128,1024]{2,1,0:T(8,128)(2,1)S(1)}, u32[]{:S(2)}, u32[]{:S(2)}) async-start(bf16[4,128,1024]{2,1,0:T(8,128)(2,1)} %get-tuple-element.22), calls=%async_computation.5 | async-start | bytes 2097152 | tf_op jit(solution)/shard_map/all_to_all | solution.py:185
  331.7 26.0 %all-to-all-done.5 = bf16[4,128,1024]{2,1,0:T(8,128)(2,1)S(1)} async-done(((bf16[4,128,1024]{2,1,0:T(8,128)(2,1)}), bf16[4,128,1024]{2,1,0:T(8,128)(2,1)S(1)}, u32[]{:S(2)}, u32[]{:S(2)}) %all-to-all-start.5) | async-done | bytes 1048608 | tf_op jit(solution)/shard_map/all_to_all | solution.py:185
  358.0 0.9 select_select_fusion
  (86 shorter events, 12.1 us)
Async XLA Ops:
  6.5 8.7 %copy-start.3 = (bf16[1,1,512,768]{3,2,1,0:T(8,128)(2,1)S(1)}, bf16[1,1,512,768]{3,2,1,0:T(8,128)(2,1)}, u32[]{:S(2)}) copy-start(bf16[1,1,512,768]{3,2,1,0:T(8,128)(2,1)} %param.14) | copy-start | bytes 2359300
  7.6 7.9 %copy-start.1 = (bf16[1,1,512,768]{3,2,1,0:T(8,128)(2,1)S(1)}, bf16[1,1,512,768]{3,2,1,0:T(8,128)(2,1)}, u32[]{:S(2)}) copy-start(bf16[1,1,512,768]{3,2,1,0:T(8,128)(2,1)} %param.15) | copy-start | bytes 2359300
  8.8 7.4 %copy-start.8 = (f32[1,4096]{1,0:T(1,128)S(1)}, f32[1,4096]{1,0:T(1,128)}, u32[]{:S(2)}) copy-start(f32[1,4096]{1,0:T(1,128)} %param.11) | copy-start | bytes 49156
  8.8 8.1 %copy-start.7 = (bf16[1,1,768,512]{3,2,1,0:T(8,128)(2,1)S(1)}, bf16[1,1,768,512]{3,2,1,0:T(8,128)(2,1)}, u32[]{:S(2)}) copy-start(bf16[1,1,768,512]{3,2,1,0:T(8,128)(2,1)} %param.16) | copy-start | bytes 2359300
  8.8 32.2 %all-to-all-start = ((bf16[4,128,1024]{2,1,0:T(8,128)(2,1)}), bf16[4,128,1024]{2,1,0:T(8,128)(2,1)S(1)}, u32[]{:S(2)}, u32[]{:S(2)}) async-start(bf16[4,128,1024]{2,1,0:T(8,128)(2,1)} %broadcast_in_dim.103), calls=%async_computation | async-start | bytes 2097152 | tf_op jit(solution)/shard_map/all_to_all | solution.py:165
  15.3 53.6 %all-gather.4.cloned.1.call-start = ((), (), s32[]{:S(2)}) async-start(), calls=%async_computation.6 | async-start | bytes 1310720 | tf_op jit(solution)/shard_map/all_gather | solution.py:181
  17.2 16.9 %copy-start.10 = (f32[1,2,128]{2,1,0:T(2,128)S(1)}, f32[1,2,128]{2,1,0:T(2,128)}, u32[]{:S(2)}) copy-start(f32[1,2,128]{2,1,0:T(2,128)} %param.17) | copy-start | bytes 3076
  17.2 16.9 %copy-start.9 = (f32[1,1,2,512]{3,2,1,0:T(2,128)S(1)}, f32[1,1,2,512]{3,2,1,0:T(2,128)}, u32[]{:S(2)}) copy-start(f32[1,1,2,512]{3,2,1,0:T(2,128)} %param.13) | copy-start | bytes 12292
  52.1 3.4 copy-start.2
  52.1 3.4 copy-start.4
  52.9 133.7 %all-gather.6.cloned.1.call-start = ((), (), s32[]{:S(2)}) async-start(), calls=%async_computation.7 | async-start | bytes 1310720 | tf_op jit(solution)/shard_map/all_gather | solution.py:181
  54.2 3.2 copy-start.11
  91.8 31.1 %copy-start = (bf16[2,128,1024]{2,1,0:T(8,128)(2,1)S(1)}, bf16[2,128,1024]{2,1,0:T(8,128)(2,1)}, u32[]{:S(2)}) copy-start(bf16[2,128,1024]{2,1,0:T(8,128)(2,1)} %param.10) | copy-start | bytes 1572868
  122.9 8.2 %collective-permute-start = (bf16[128,1024]{1,0:T(8,128)(2,1)S(1)}, bf16[128,1024]{1,0:T(8,128)(2,1)S(1)}, u32[]{:S(2)}, u32[]{:S(2)}) collective-permute-start(bf16[128,1024]{1,0:T(8,128)(2,1)S(1)} %add_convert_fusion.2), channel_id=1, source_target_pairs={{0,16},{1,17},{2,18},{3,19},{4,20},{5,21},{6,22},{7,23},{8,24},{9,... | collective-permute-start | bytes 786440 | tf_op jit(solution)/shard_map/ppermute | solution.py:22
  170.5 133.5 %all-gather.8.cloned.1.call-start = ((), (), s32[]{:S(2)}) async-start(), calls=%async_computation.8 | async-start | bytes 1310720 | tf_op jit(solution)/shard_map/all_gather | solution.py:181
  240.5 8.2 %copy-start.5 = (bf16[128,1024]{1,0:T(8,128)(2,1)}, bf16[128,1024]{1,0:T(8,128)(2,1)S(1)}, u32[]{:S(2)}) copy-start(bf16[128,1024]{1,0:T(8,128)(2,1)S(1)} %add_convert_fusion.1) | copy-start | bytes 786436
  240.5 8.2 %collective-permute-start.1 = (bf16[128,1024]{1,0:T(8,128)(2,1)S(1)}, bf16[128,1024]{1,0:T(8,128)(2,1)S(1)}, u32[]{:S(2)}, u32[]{:S(2)}) collective-permute-start(bf16[128,1024]{1,0:T(8,128)(2,1)S(1)} %add_convert_fusion.1), channel_id=1, source_target_pairs={{0,16},{1,17},{2,18},{3,19},{4,20},{5,21},{6,22},{7,23},{8,24},{9,... | collective-permute-start | bytes 786440 | tf_op jit(solution)/shard_map/ppermute | solution.py:22
  327.0 30.7 %all-to-all-start.5 = ((bf16[4,128,1024]{2,1,0:T(8,128)(2,1)}), bf16[4,128,1024]{2,1,0:T(8,128)(2,1)S(1)}, u32[]{:S(2)}, u32[]{:S(2)}) async-start(bf16[4,128,1024]{2,1,0:T(8,128)(2,1)} %get-tuple-element.22), calls=%async_computation.5 | async-start | bytes 2097152 | tf_op jit(solution)/shard_map/all_to_all | solution.py:185
  331.6 26.4 %copy-start.6 = (bf16[128,1024]{1,0:T(8,128)(2,1)S(1)}, bf16[128,1024]{1,0:T(8,128)(2,1)}, u32[]{:S(2)}) copy-start(bf16[128,1024]{1,0:T(8,128)(2,1)} %copy-done.5) | copy-start | bytes 786436
Sparse Core Ops, SparseCore 0:
  53.0 15.7 all-gather.3
  170.7 15.8 all-gather.5
  288.2 15.8 all-gather.7

commit v3 on v2

--- a/solution.py
+++ b/solution.py
@@ -1,3 +1,5 @@
+import functools
+
 import jax
 import jax.numpy as jnp
 from jax import lax
@@ -14,12 +16,6 @@
 update_step = 1.0
 norm_eps = 1e-06
 grad_eps = 1e-07
-
-
-def shifted(array, axis, by):
-    devices = lax.axis_size(axis)
-    pairs = [(i, i + by) for i in range(devices) if 0 <= i + by < devices]
-    return lax.ppermute(array, axis, pairs)
 
 
 def rms_scale(values):
@@ -159,6 +155,332 @@
     )(active, both, queries, *fasts, *norms, out_gain_row, out_weights)
 
 
+def signal(semaphore, target):
+    pl.semaphore_signal(
+        semaphore, inc=1, device_id=target, device_id_type=pl.DeviceIdType.MESH
+    )
+
+
+def remote(source, target, send_sem, recv_sem, device):
+    return pltpu.make_async_remote_copy(
+        src_ref=source,
+        dst_ref=target,
+        send_sem=send_sem,
+        recv_sem=recv_sem,
+        device_id=device,
+        device_id_type=pl.DeviceIdType.MESH,
+    )
+
+
+def gather_tokens_kernel(devices, own_ref, all_ref, send_sems, recv_sems, pair_sends, pair_recvs, own_sem):
+    me = lax.axis_index("seq")
+    chips = devices // 2
+    chip, core = me // 2, lax.rem(me, 2)
+    partner = {"seq": 2 * chip + 1 - core}
+    parts, rows = own_ref.shape[0], own_ref.shape[1]
+    barrier = pltpu.get_barrier_semaphore()
+    signal(barrier, partner)
+    for step in range(1, chips):
+        signal(barrier, {"seq": 2 * lax.rem(chip + step, chips) + core})
+    pl.semaphore_wait(barrier, chips)
+
+    def place(part, origin):
+        return all_ref.at[part, pl.ds(pl.multiple_of(origin * rows, rows), rows), :]
+
+    far, near = {}, {}
+    for part in range(parts):
+        for step in range(1, chips):
+            far[part, step] = remote(
+                own_ref.at[part],
+                place(part, me),
+                send_sems.at[part, step],
+                recv_sems.at[part, step],
+                {"seq": 2 * lax.rem(chip + step, chips) + core},
+            )
+            far[part, step].start()
+        near[part, 0] = remote(
+            own_ref.at[part], place(part, me), pair_sends.at[part, 0], pair_recvs.at[part, 0], partner
+        )
+        near[part, 0].start()
+    copies = []
+    for part in range(parts):
+        copies.append(pltpu.make_async_copy(own_ref.at[part], place(part, me), own_sem.at[part]))
+        copies[-1].start()
+    for part in range(parts):
+        for step in range(1, chips):
+            far[part, step].wait_recv()
+            origin = 2 * lax.rem(chip + chips - step, chips) + core
+            near[part, step] = remote(
+                place(part, origin),
+                place(part, origin),
+                pair_sends.at[part, step],
+                pair_recvs.at[part, step],
+                partner,
+            )
+            near[part, step].start()
+    for copy in copies:
+        copy.wait()
+    for copy in far.values():
+        copy.wait_send()
+    for copy in near.values():
+        copy.wait_send()
+        copy.wait_recv()
+
+
+def gather_tokens(own):
+    devices = lax.axis_size("seq")
+    parts, rows, width = own.shape
+    vmem = pl.BlockSpec(memory_space=pltpu.VMEM)
+    return pl.pallas_call(
+        functools.partial(gather_tokens_kernel, devices),
+        name="gather_tokens",
+        out_shape=jax.ShapeDtypeStruct((parts, devices * rows, width), own.dtype),
+        in_specs=[vmem],
+        out_specs=vmem,
+        scratch_shapes=[pltpu.SemaphoreType.DMA((parts, devices // 2))] * 4
+        + [pltpu.SemaphoreType.DMA((parts,))],
+        compiler_params=pltpu.CompilerParams(
+            collective_id=0, has_side_effects=True, vmem_limit_bytes=16 * 1024 * 1024
+        ),
+    )(own)
+
+
+def exchange_kernel(heads, segments, chunks, onward, *refs):
+    if onward:
+        terms_ref, residual_ref, stream_ref, result_ref, whole_ref = refs[:5]
+        slots, total, sum_sends, sum_recvs, copy_sends, copy_recvs, hop_sends, hop_recvs, own_sem = refs[5:]
+    else:
+        terms_ref, residual_ref, result_ref, slots, total, sum_sends, sum_recvs = refs
+    me = lax.axis_index("head")
+    segment = lax.axis_index("segment")
+    rows, width = residual_ref.shape
+    piece = rows // chunks
+    has_left, has_right = me >= 1, me + 1 < heads
+    barrier = pltpu.get_barrier_semaphore()
+    awaited = has_left.astype(jnp.int32) + has_right.astype(jnp.int32)
+
+    @pl.when(has_left)
+    def _():
+        signal(barrier, {"head": me - 1})
+
+    @pl.when(has_right)
+    def _():
+        signal(barrier, {"head": me + 1})
+
+    if onward:
+        awaited = awaited + (segment + 1 < segments).astype(jnp.int32)
+
+        @pl.when(segment >= 1)
+        def _():
+            signal(barrier, {"segment": segment - 1})
+
+    pl.semaphore_wait(barrier, awaited)
+
+    def rows_of(chunk):
+        return pl.ds(chunk * piece, piece)
+
+    def within(position):
+        return (position >= 0) & (position < heads)
+
+    sides = ((0, 1), (1, -1))
+
+    def sum_copy(side, sign, distance, chunk, first):
+        source = (
+            terms_ref.at[me + sign * distance, rows_of(chunk), :]
+            if first
+            else slots.at[side, distance, rows_of(chunk), :]
+        )
+        return remote(
+            source,
+            slots.at[side, distance - 1, rows_of(chunk), :],
+            sum_sends.at[side, distance, chunk],
+            sum_recvs.at[side, distance - 1, chunk],
+            {"head": me + sign},
+        )
+
+    def sum_arrival(side, sign, distance, chunk):
+        return remote(
+            slots.at[side, distance, rows_of(chunk), :],
+            slots.at[side, distance, rows_of(chunk), :],
+            sum_sends.at[side, distance, chunk],
+            sum_recvs.at[side, distance, chunk],
+            {"head": me - sign},
+        )
+
+    def send_sums(distance, chunk):
+        for side, sign in sides:
+
+            @pl.when(within(me + sign * distance) & jnp.logical_not(within(me - sign)))
+            def _():
+                sum_copy(side, sign, distance, chunk, True).start()
+
+            if distance < heads - 1:
+
+                @pl.when(within(me + sign * distance) & within(me - sign))
+                def _():
+                    sum_arrival(side, sign, distance, chunk).wait_recv()
+                    here = rows_of(chunk)
+                    slots[side, distance, here, :] = (
+                        slots[side, distance, here, :].astype(jnp.float32)
+                        + terms_ref[me + sign * distance, here, :].astype(jnp.float32)
+                    ).astype(jnp.bfloat16)
+                    sum_copy(side, sign, distance, chunk, False).start()
+
+    def finish(chunk):
+        here = rows_of(chunk)
+        total[...] = residual_ref[here, :].astype(jnp.float32) + terms_ref[me, here, :].astype(
+            jnp.float32
+        )
+        for side, sign in sides:
+
+            @pl.when(within(me - sign))
+            def _():
+                sum_arrival(side, sign, 0, chunk).wait_recv()
+                total[...] += slots[side, 0, here, :].astype(jnp.float32)
+
+        result_ref[here, :] = total[...].astype(jnp.bfloat16)
+        if onward:
+
+            @pl.when(segment + 1 < segments)
+            def _():
+                hop(chunk).start()
+
+    def place(origin, chunk):
+        return whole_ref.at[
+            rows_of(chunk), pl.ds(pl.multiple_of(origin * width, width), width)
+        ]
+
+    def hop(chunk):
+        return remote(
+            result_ref.at[rows_of(chunk), :],
+            place(me, chunk),
+            hop_sends.at[chunk],
+            hop_recvs.at[chunk],
+            {"segment": segment + 1},
+        )
+
+    def hop_arrival(chunk):
+        return remote(
+            place(me, chunk),
+            place(me, chunk),
+            hop_sends.at[chunk],
+            hop_recvs.at[chunk],
+            {"segment": segment - 1},
+        )
+
+    def block_copy(side, sign, step, chunk):
+        origin = me - sign * step
+        return remote(
+            place(origin, chunk),
+            place(origin, chunk),
+            copy_sends.at[side, step, chunk],
+            copy_recvs.at[side, step, chunk],
+            {"head": me + sign},
+        )
+
+    def block_arrival(side, sign, step, chunk):
+        origin = me - sign * (step + 1)
+        return remote(
+            place(origin, chunk),
+            place(origin, chunk),
+            copy_sends.at[side, step, chunk],
+            copy_recvs.at[side, step, chunk],
+            {"head": me - sign},
+        )
+
+    def send_blocks(step, chunk):
+        if step == 0:
+
+            @pl.when(segment >= 1)
+            def _():
+                hop_arrival(chunk).wait_recv()
+
+        for side, sign in sides:
+            if step > 0:
+
+                @pl.when(within(me - sign * step))
+                def _():
+                    block_arrival(side, sign, step - 1, chunk).wait_recv()
+
+            if step < heads - 1:
+
+                @pl.when(within(me - sign * step) & within(me + sign))
+                def _():
+                    block_copy(side, sign, step, chunk).start()
+
+    if onward:
+        own = pltpu.make_async_copy(
+            stream_ref, whole_ref.at[:, pl.ds(pl.multiple_of(me * width, width), width)], own_sem
+        )
+
+        @pl.when(segment == 0)
+        def _():
+            own.start()
+            own.wait()
+
+    stages = [functools.partial(send_sums, distance) for distance in range(heads - 1, 0, -1)]
+    stages.append(finish)
+    if onward:
+        stages += [functools.partial(send_blocks, step) for step in range(heads)]
+    for moment in range(chunks + len(stages) - 1):
+        for index, stage in enumerate(stages):
+            if 0 <= moment - index < chunks:
+                stage(moment - index)
+
+    for chunk in range(chunks):
+        for side, sign in sides:
+            for distance in range(1, heads):
+
+                @pl.when(within(me + sign * distance))
+                def _():
+                    sum_copy(side, sign, distance, chunk, True).wait_send()
+
+            if onward:
+                for step in range(heads - 1):
+
+                    @pl.when(within(me - sign * step) & within(me + sign))
+                    def _():
+                        block_copy(side, sign, step, chunk).wait_send()
+
+        if onward:
+
+            @pl.when(segment + 1 < segments)
+            def _():
+                hop(chunk).wait_send()
+
+
+def exchange(terms, residual, following):
+    heads, rows, width = terms.shape
+    segments = lax.axis_size("segment")
+    onward = following is not None
+    chunks = 4
+    vmem = pl.BlockSpec(memory_space=pltpu.VMEM)
+    shapes = [jax.ShapeDtypeStruct((rows, width), jnp.bfloat16)]
+    scratch = [
+        pltpu.VMEM((2, heads, rows, width), jnp.bfloat16),
+        pltpu.VMEM((rows // chunks, width), jnp.float32),
+    ] + [pltpu.SemaphoreType.DMA((2, heads, chunks))] * 2
+    operands = [terms, residual]
+    if onward:
+        operands.append(following)
+        shapes.append(jax.ShapeDtypeStruct((rows, heads * width), jnp.bfloat16))
+        scratch += [pltpu.SemaphoreType.DMA((2, heads, chunks))] * 2
+        scratch += [pltpu.SemaphoreType.DMA((chunks,))] * 2 + [pltpu.SemaphoreType.DMA]
+    return pl.pallas_call(
+        functools.partial(exchange_kernel, heads, segments, chunks, onward),
+        name="exchange" if onward else "reduce",
+        out_shape=tuple(shapes),
+        in_specs=[vmem] * len(operands),
+        out_specs=(vmem,) * len(shapes),
+        scratch_shapes=scratch,
+        compiler_params=pltpu.CompilerParams(
+            collective_id=1 if onward else 2,
+            has_side_effects=True,
+            vmem_limit_bytes=24 * 1024 * 1024,
+        ),
+    )(*operands)
+
+
 def gather_heads(block):
     heads = lax.axis_size("head")
     spread = jnp.broadcast_to(block[None], (heads,) + block.shape)
@@ -166,25 +488,18 @@
 
 
 def run_section(
-    residual, gain_row, qkv_matrix, head_gains, rate_row, out_gain_row, out_weights, fasts, norms, active
+    whole, gain_row, qkv_matrix, head_gains, rate_row, out_gain_row, out_weights, fasts, norms, active
 ):
-    values = residual.astype(jnp.float32)
-    rows, width = residual.shape
+    rows = whole.shape[0]
     heads = lax.axis_size("head")
     head_width = head_gains.shape[-1]
-    whole = gather_heads(residual).swapaxes(0, 1).reshape(rows, heads * width)
     normed = (rms_scale(whole.astype(jnp.float32)) * gain_row).astype(jnp.bfloat16)
     projected = dot(normed, qkv_matrix).reshape(rows, 3, head_width)
     queries = (rms_scale(projected[:, 0]) * head_gains[0]).astype(jnp.bfloat16)
     key_rows = (rms_scale(projected[:, 1]) * head_gains[1]).astype(jnp.bfloat16)
     out_grad = (-rate_row[:, None] * projected[:, 2]).astype(jnp.bfloat16)
-    both = lax.all_gather(jnp.stack([key_rows, out_grad]), "seq", axis=1, tiled=True)
-    terms, *fasts = fast_step(
-        active, both, queries, fasts, norms, out_gain_row, out_weights, heads
-    )
-    parts = lax.all_to_all(terms, "head", split_axis=0, concat_axis=0, tiled=True)
-    delta = jnp.sum(parts.astype(jnp.float32), axis=0)
-    return ((values + delta).astype(jnp.bfloat16), tuple(fasts))
+    both = gather_tokens(jnp.stack([key_rows, out_grad]))
+    return fast_step(active, both, queries, fasts, norms, out_gain_row, out_weights, heads)
 
 
 def shards(stream, in_gain, w_qkv, qk_gain, w_one, w_three, w_two, token_rate, out_gain, w_out):
@@ -201,16 +516,16 @@
         jnp.stack([jnp.sqrt(jnp.sum(matrix * matrix, axis=0, keepdims=True)) for matrix in fasts[:2]]),
         jnp.sqrt(jnp.sum(fasts[2] * fasts[2], axis=1, keepdims=True)),
     )
-    received = jnp.zeros_like(stream[0])
     collected = jnp.zeros(stream.shape, jnp.bfloat16)
+    source = stream[0]
+    whole = gather_heads(source).swapaxes(0, 1).reshape(source.shape[0], -1)
     for moment in range(moments):
         span_index = moment - segment_index
         active = (span_index >= 0) & (span_index < span_count)
         clipped = jnp.clip(span_index, 0, span_count - 1)
-        source = jnp.where(segment_index == 0, stream[min(moment, span_count - 1)], received)
         rate_row = lax.dynamic_index_in_dim(token_rate[0], clipped, 0, keepdims=False)
-        result, fasts = run_section(
-            source,
+        terms, *fasts = run_section(
+            whole,
             in_gain[0],
             qkv_matrix,
             qk_gain[0, 0],
@@ -221,10 +536,16 @@
             norms,
             active.astype(jnp.int32)[None],
         )
+        if moment + 1 < moments:
+            following = stream[min(moment + 1, span_count - 1)]
+            result, whole = exchange(terms, source, following)
+            source = lax.dynamic_slice_in_dim(
+                whole, lax.axis_index("head") * source.shape[1], source.shape[1], axis=1
+            )
+        else:
+            (result,) = exchange(terms, source, None)
         chosen = jnp.arange(span_count) == span_index
         collected = jnp.where(chosen[:, None, None], result[None], collected)
-        if moment + 1 < moments:
-            received = shifted(result, "segment", 1)
     return collected[None]
 
 

time: 366 us -> 269 us (0.73)
  Pallas kernels: 68.8 us -> 193 us
  blocking collectives: 116 us -> 0 us
  waiting for transfers between devices: 83 us -> 1.36 us
  between operations: 13.5 us -> 0.42 us
  starting transfers between devices: 18.3 us -> 6.48 us
  local copies, waits for them, and re-layouts: 22.1 us -> 29.4 us
  other arithmetic: 16.6 us -> 10.6 us
    pallas_call x0 -> x6, Pallas kernels: none -> 124 us  [the longest x3 95.9 us: exchange(): pl.pallas_call(functools.partial(exchange_kernel, heads, segments, chunks...]
    all_to_all x4 -> x0, blocking collectives: 116 us -> none  [the longest x2 61.6 us: run_section(): lax.all_to_all(terms, 'head', split_axis=0, concat_axis=0, tiled=True)]
    all_gather x3 -> x0, waiting for transfers between devices: 40.5 us -> none  [run_section(): lax.all_gather(jnp.stack([key_rows, out_grad]), 'seq', axis=1, tiled=True)]
    all_to_all x1 -> x0, waiting for transfers between devices: 26 us -> none  [run_section(): lax.all_to_all(terms, 'head', split_axis=0, concat_axis=0, tiled=True)]
    ppermute x2 -> x0, waiting for transfers between devices: 9.63 us -> none  [shifted(): return lax.ppermute(array, axis, pairs)]
    unnamed x28 -> x30, local copies, waits for them, and re-layouts: 17.8 us -> 25.6 us
    ppermute x2 -> x0, starting transfers between devices: 6.78 us -> none  [shifted(): return lax.ppermute(array, axis, pairs)]
    all_to_all x1, waiting for transfers between devices: 6.81 us -> 1.36 us  [gather_heads(): lax.all_to_all(spread, 'head', split_axis=0, concat_axis=0, tiled=True)]
  transfers between devices with their start and end apart: 7 -> 1, of which waited for: 7 -> 1; matrix products, arithmetic and copies ran while one was open for 7% -> 9% of each run, Pallas kernels for 0% -> 0%
where the time goes in v3:
time: 269 us; the launch traced here: 268 us
  Pallas kernels  193 us (72%)
  local copies, waits for them, and re-layouts  29.4 us (11%)
  matrix products  26.7 us (10%)
  other arithmetic  10.6 us (4%)
  starting transfers between devices  6.48 us (2%)
    pallas_call x3, Pallas kernels, exchange(): pl.pallas_call(functools.partial(exchange_kernel, heads, segments, chunks...  95.9 us
    pallas_call x3, Pallas kernels, fast_step(): pl.pallas_call(fast_kernel, name='fast_step', out_shape=(jax.ShapeDtypeSt...  68.8 us
    pallas_call x3, Pallas kernels, gather_tokens(): pl.pallas_call(functools.partial(gather_tokens_kernel, devices), name='ga...  28 us
    dot_general x3, matrix products, dot(): return jnp.dot(left, right, preferred_element_type=jnp.float32)  26.7 us
    unnamed x30, local copies, waits for them, and re-layouts  25.6 us
    all_to_all x1, starting transfers between devices, gather_heads(): lax.all_to_all(spread, 'head', split_axis=0, concat_axis=0, tiled=True)  6.48 us
  transfers between devices with their start and end apart: 1, of which 1 were waited for; matrix products, arithmetic and copies ran while one was open for 9% of the time, Pallas kernels for 0%

profile of v3, /device:TPU:0, one launch (start us, length us, event | category | flops | bytes accessed | tf_op | source)
XLA Modules:
  0.0 267.7 jit_solution(6346177644508302598)
XLA Ops:
  0.0 1.1 slice_bitcast_fusion.6
  1.2 1.1 broadcast_in_dim.91
  2.3 6.5 %all-to-all-start = ((bf16[4,128,1024]{2,1,0:T(8,128)(2,1)}), bf16[4,128,1024]{2,1,0:T(8,128)(2,1)S(1)}, u32[]{:S(2)}, u32[]{:S(2)}) async-start(bf16[4,128,1024]{2,1,0:T(8,128)(2,1)} %broadcast_in_dim.91), calls=%async_computation | async-start | bytes 2097152 | tf_op jit(solution)/shard_map/all_to_all | solution.py:487
  10.4 1.4 copy.25
  12.0 0.9 copy.26.down_norm_ref
  12.9 16.9 %copy.23 = bf16[1,4096,1,3,512]{1,4,3,2,0:T(8,128)(2,1)} copy(bf16[1,4096,1,3,512]{4,1,3,2,0:T(8,128)(2,1)} %param.12) | data formatting | bytes 25165824 | tf_op args[2]
  30.0 1.3 convert_bitcast_fusion.down_ref
  31.2 1.9 bitcast_convert_fusion
  33.1 1.4 all-to-all-done
  35.7 0.7 fusion.8
  36.4 8.9 %fusion.4 = f32[128,3,512]{2,0,1:T(8,128)S(1)} fusion(bf16[128,4096,1]{0,1,2:T(8,128)(2,1)S(1)} %bitcast.115, bf16[1,4096,1,3,512]{1,4,3,2,0:T(8,128)(2,1)} %copy.23), kind=kOutput, calls=%fused_computation.4 | convolution fusion | flops 1610612736 | bytes 14417920 | tf_op jit(solution)/shard_map/dot_general | solution.py:26
  45.7 9.7 %gather_tokens.3.both_ref = bf16[2,512,512]{2,1,0:T(8,128)(2,1)S(1)} custom-call(bf16[2,128,512]{2,1,0:T(8,128)(2,1)S(1)} %pad_maximum_fusion.own_ref), custom_call_target="tpu_custom_call" | custom-call | tf_op jit(solution)/shard_map/gather_tokens/pallas_call | solution.py:234
  55.5 1.0 copy-done
  56.5 0.7 multiply_convert_fusion.2.query_ref
  57.2 22.9 %fast_step.3 = (bf16[4,128,1024]{2,1,0:T(8,128)(2,1)}, f32[512,768]{1,0:T(8,128)}, f32[512,768]{1,0:T(8,128)}, f32[512,768]{1,0:T(8,128)}) custom-call(s32[1]{0:T(128)} %bitcast.2.active_ref, bf16[2,512,512]{2,1,0:T(8,128)(2,1)} %copy-done, bf16[128,512]{1,0:T(8,128)(2,1)} %multiply_convert_fusion.2.query_ref, f32[512,768]{1,0:T(8,128)} %get-tuple-element.45.gate_ref, ...), custom_call_target="tpu_custom_call" | custom-call | flops 10000000000 | bytes 20000000 | tf_op jit(solution)/shard_map/fast_step/pallas_call | solution.py:137
  80.1 1.2 copy-done.3
  81.3 37.8 %exchange.2 = (bf16[128,1024]{1,0:T(8,128)(2,1)S(1)}, bf16[128,4096]{1,0:T(8,128)(2,1)S(1)}) custom-call(bf16[4,128,1024]{2,1,0:T(8,128)(2,1)S(1)} %copy-done.3, bf16[128,1024]{1,0:T(8,128)(2,1)S(1)} %get-tuple-element.38.refs_1_, bf16[128,1024]{1,0:T(8,128)(2,1)S(1)} %get-tuple-element.37.refs_2_), custom_call_target="tpu_custom_call" | custom-call | tf_op jit(solution)/shard_map/exchange/pallas_call | solution.py:469
  119.5 8.9 %fusion.2 = f32[128,3,512]{2,0,1:T(8,128)S(1)} fusion(bf16[1,4096,1,3,512]{1,4,3,2,0:T(8,128)(2,1)} %copy.23, bf16[128,4096]{1,0:T(8,128)(2,1)S(1)} %get-tuple-element.19, f32[4096]{0:T(1024)S(1)} %bitcast.116, f32[128]{0:T(128)S(1)} %add_rsqrt_fusion.5), kind=kOutput, calls=%fused_computation.2 | convolution fusion | flops 1612709888 | bytes 14434816 | tf_op jit(solution)/shard_map/dot_general | solution.py:26
  128.7 0.7 multiply_convert_fusion.1.query_ref
  129.5 8.6 %gather_tokens.4.both_ref = bf16[2,512,512]{2,1,0:T(8,128)(2,1)S(1)} custom-call(bf16[2,128,512]{2,1,0:T(8,128)(2,1)S(1)} %pad_maximum_fusion.1.own_ref), custom_call_target="tpu_custom_call" | custom-call | tf_op jit(solution)/shard_map/gather_tokens/pallas_call | solution.py:234
  138.2 1.0 copy-done.2
  139.2 22.9 %fast_step.4 = (bf16[4,128,1024]{2,1,0:T(8,128)(2,1)}, f32[512,768]{1,0:T(8,128)}, f32[512,768]{1,0:T(8,128)}, f32[512,768]{1,0:T(8,128)}) custom-call(s32[1]{0:T(128)} %bitcast.1.active_ref, bf16[2,512,512]{2,1,0:T(8,128)(2,1)} %copy-done.2, bf16[128,512]{1,0:T(8,128)(2,1)} %multiply_convert_fusion.1.query_ref, f32[512,768]{1,0:T(8,128)} %get-tuple-element.20.gate_ref, ...), custom_call_target="tpu_custom_call" | custom-call | flops 10000000000 | bytes 20000000 | tf_op jit(solution)/shard_map/fast_step/pallas_call | solution.py:137
  162.2 1.2 copy-done.4
  163.4 37.5 %exchange.3 = (bf16[128,1024]{1,0:T(8,128)(2,1)S(1)}, bf16[128,4096]{1,0:T(8,128)(2,1)S(1)}) custom-call(bf16[4,128,1024]{2,1,0:T(8,128)(2,1)S(1)} %copy-done.4, bf16[128,1024]{1,0:T(8,128)(2,1)S(1)} %constant_dynamic-slice_fusion.2.refs_1_, bf16[128,1024]{1,0:T(8,128)(2,1)S(1)} %get-tuple-element.37.refs_2_), custom_call_target="tpu_custom_call" | custom-call | tf_op jit(solution)/shard_map/exchange/pallas_call | solution.py:469
  201.3 8.9 %fusion = f32[128,3,512]{2,0,1:T(8,128)S(1)} fusion(bf16[1,4096,1,3,512]{1,4,3,2,0:T(8,128)(2,1)} %copy.23, bf16[128,4096]{1,0:T(8,128)(2,1)S(1)} %get-tuple-element.24, f32[128]{0:T(128)S(1)} %add_rsqrt_fusion.2, f32[4096]{0:T(1024)S(1)} %bitcast.117), kind=kOutput, calls=%fused_computation | convolution fusion | flops 1612709888 | bytes 14434816 | tf_op jit(solution)/shard_map/dot_general | solution.py:26
  210.4 0.7 multiply_convert_fusion.query_ref
  211.3 9.7 %gather_tokens.5.both_ref = bf16[2,512,512]{2,1,0:T(8,128)(2,1)S(1)} custom-call(bf16[2,128,512]{2,1,0:T(8,128)(2,1)S(1)} %pad_maximum_fusion.2.own_ref), custom_call_target="tpu_custom_call" | custom-call | tf_op jit(solution)/shard_map/gather_tokens/pallas_call | solution.py:234
  221.0 1.0 copy-done.1
  222.1 22.9 %fast_step.5 = (bf16[4,128,1024]{2,1,0:T(8,128)(2,1)}, f32[512,768]{1,0:T(8,128)}, f32[512,768]{1,0:T(8,128)}, f32[512,768]{1,0:T(8,128)}) custom-call(s32[1]{0:T(128)} %bitcast.active_ref, bf16[2,512,512]{2,1,0:T(8,128)(2,1)} %copy-done.1, bf16[128,512]{1,0:T(8,128)(2,1)} %multiply_convert_fusion.query_ref, f32[512,768]{1,0:T(8,128)} %get-tuple-element.25.gate_ref, ...), custom_call_target="tpu_custom_call" | custom-call | flops 10000000000 | bytes 20000000 | tf_op jit(solution)/shard_map/fast_step/pallas_call | solution.py:137
  245.0 1.2 copy-done.5
  246.2 20.5 %reduce.10 = bf16[128,1024]{1,0:T(8,128)(2,1)S(1)} custom-call(bf16[4,128,1024]{2,1,0:T(8,128)(2,1)S(1)} %copy-done.5, bf16[128,1024]{1,0:T(8,128)(2,1)S(1)} %constant_dynamic-slice_fusion.refs_1_), custom_call_target="tpu_custom_call" | custom-call | tf_op jit(solution)/shard_map/reduce/pallas_call | solution.py:469
  266.7 0.9 select_select_fusion
  (62 shorter events, 4.9 us)
Async XLA Ops:
  0.0 8.7 %copy-start.7 = (bf16[1,1,512,768]{3,2,1,0:T(8,128)(2,1)S(1)}, bf16[1,1,512,768]{3,2,1,0:T(8,128)(2,1)}, u32[]{:S(2)}) copy-start(bf16[1,1,512,768]{3,2,1,0:T(8,128)(2,1)} %param.14) | copy-start | bytes 2359300
  1.1 7.8 %copy-start.6 = (bf16[1,1,512,768]{3,2,1,0:T(8,128)(2,1)S(1)}, bf16[1,1,512,768]{3,2,1,0:T(8,128)(2,1)}, u32[]{:S(2)}) copy-start(bf16[1,1,512,768]{3,2,1,0:T(8,128)(2,1)} %param.15) | copy-start | bytes 2359300
  2.3 7.4 %copy-start.9 = (f32[1,4096]{1,0:T(1,128)S(1)}, f32[1,4096]{1,0:T(1,128)}, u32[]{:S(2)}) copy-start(f32[1,4096]{1,0:T(1,128)} %param.11) | copy-start | bytes 49156
  2.3 32.2 %all-to-all-start = ((bf16[4,128,1024]{2,1,0:T(8,128)(2,1)}), bf16[4,128,1024]{2,1,0:T(8,128)(2,1)S(1)}, u32[]{:S(2)}, u32[]{:S(2)}) async-start(bf16[4,128,1024]{2,1,0:T(8,128)(2,1)} %broadcast_in_dim.91), calls=%async_computation | async-start | bytes 2097152 | tf_op jit(solution)/shard_map/all_to_all | solution.py:487
  12.9 17.0 %copy-start.11 = (f32[1,2,128]{2,1,0:T(2,128)S(1)}, f32[1,2,128]{2,1,0:T(2,128)}, u32[]{:S(2)}) copy-start(f32[1,2,128]{2,1,0:T(2,128)} %param.17) | copy-start | bytes 3076
  12.9 17.0 %copy-start.10 = (f32[1,1,2,512]{3,2,1,0:T(2,128)S(1)}, f32[1,1,2,512]{3,2,1,0:T(2,128)}, u32[]{:S(2)}) copy-start(f32[1,1,2,512]{3,2,1,0:T(2,128)} %param.13) | copy-start | bytes 12292
  29.8 1.4 copy-start.8
  29.9 3.2 %copy-start.12 = (f32[2,1,768]{2,1,0:T(1,128)}, f32[2,1,768]{2,1,0:T(1,128)S(1)}, u32[]{:S(2)}) copy-start(f32[2,1,768]{2,1,0:T(1,128)S(1)} %constant_dynamic-update-slice_fusion.wide_norms_ref) | copy-start | bytes 18436
  55.4 1.0 copy-start
  80.1 1.2 copy-start.3
  138.2 1.0 copy-start.2
  162.2 1.2 copy-start.4
  221.0 1.0 copy-start.1
  245.0 1.2 copy-start.5

commit v4 on v3

--- a/solution.py
+++ b/solution.py
@@ -134,6 +134,7 @@
     width = out_weights.shape[1] // heads
     vmem = pl.BlockSpec(memory_space=pltpu.VMEM)
     state = jax.ShapeDtypeStruct((inner, wide), jnp.float32)
+    held = 4 * both.size + 6 * both.shape[1] * wide + 30 * inner * wide + 2 * out_weights.size
     return pl.pallas_call(
         fast_kernel,
         name="fast_step",
@@ -148,7 +149,7 @@
             pltpu.VMEM(out_weights.shape, jnp.bfloat16),
             pltpu.SemaphoreType.DMA,
         ],
-        compiler_params=pltpu.CompilerParams(vmem_limit_bytes=60 * 1024 * 1024),
+        compiler_params=pltpu.CompilerParams(vmem_limit_bytes=held + 14 * 1024 * 1024),
         cost_estimate=pl.CostEstimate(
             flops=10**10, bytes_accessed=2 * 10**7, transcendentals=0
         ),

time: 269 us -> 251 us (0.933)
  Pallas kernels: 193 us -> 181 us
  local copies, waits for them, and re-layouts: 29.4 us -> 25.5 us
  other arithmetic: 10.6 us -> 7.55 us
    pallas_call x3, Pallas kernels: 68.8 us -> 56.9 us  [fast_step(): pl.pallas_call(fast_kernel, name='fast_step', out_shape=(jax.ShapeDtypeSt...]
    unnamed x30 -> x34, local copies, waits for them, and re-layouts: 25.6 us -> 21.3 us
where the time goes in v4:
time: 251 us; the launch traced here: 250 us
  Pallas kernels  181 us (72%)
  matrix products  26.8 us (11%)
  local copies, waits for them, and re-layouts  25.5 us (10%)
  other arithmetic  7.55 us (3%)
  starting transfers between devices  6.48 us (3%)
    pallas_call x3, Pallas kernels, exchange(): pl.pallas_call(functools.partial(exchange_kernel, heads, segments, chunks...  95.9 us
    pallas_call x3, Pallas kernels, fast_step(): pl.pallas_call(fast_kernel, name='fast_step', out_shape=(jax.ShapeDtypeSt...  56.9 us
    pallas_call x3, Pallas kernels, gather_tokens(): pl.pallas_call(functools.partial(gather_tokens_kernel, devices), name='ga...  28.1 us
    dot_general x3, matrix products, dot(): return jnp.dot(left, right, preferred_element_type=jnp.float32)  26.8 us
    unnamed x34, local copies, waits for them, and re-layouts  21.3 us
    all_to_all x1, starting transfers between devices, gather_heads(): lax.all_to_all(spread, 'head', split_axis=0, concat_axis=0, tiled=True)  6.48 us
  transfers between devices with their start and end apart: 1, of which 1 were waited for; matrix products, arithmetic and copies ran while one was open for 9% of the time, Pallas kernels for 0%

profile of v4, /device:TPU:0, one launch (start us, length us, event | category | flops | bytes accessed | tf_op | source)
XLA Modules:
  0.0 249.8 jit_solution(12727152949286967580)
XLA Ops:
  0.0 1.1 slice_bitcast_fusion.6
  1.2 1.1 broadcast_in_dim.91
  2.3 6.5 %all-to-all-start = ((bf16[4,128,1024]{2,1,0:T(8,128)(2,1)}), bf16[4,128,1024]{2,1,0:T(8,128)(2,1)}, u32[]{:S(2)}, u32[]{:S(2)}) async-start(bf16[4,128,1024]{2,1,0:T(8,128)(2,1)} %broadcast_in_dim.91), calls=%async_computation | async-start | bytes 2097152 | tf_op jit(solution)/shard_map/all_to_all | solution.py:488
  9.0 0.2 multiply_reduce_fusion.1
  9.2 0.6 broadcast.351
  9.8 0.7 reduce.9
  10.5 1.4 copy.25
  11.9 0.2 multiply_reduce_fusion
  12.4 16.9 %copy.23 = bf16[1,4096,1,3,512]{1,4,3,2,0:T(8,128)(2,1)} copy(bf16[1,4096,1,3,512]{4,1,3,2,0:T(8,128)(2,1)} %param.12) | data formatting | bytes 25165824 | tf_op args[2]
  29.5 0.9 copy-done.9
  30.4 0.2 copy-done.11
  30.7 1.9 bitcast_convert_fusion
  32.6 2.0 all-to-all-done
  34.6 1.6 copy.22
  36.2 0.6 fusion.6
  36.8 0.7 fusion.8
  37.5 9.0 %fusion.4 = f32[128,3,512]{2,0,1:T(8,128)S(1)} fusion(bf16[128,4096,1]{0,1,2:T(8,128)(2,1)S(1)} %bitcast.121, bf16[1,4096,1,3,512]{1,4,3,2,0:T(8,128)(2,1)} %copy.23), kind=kOutput, calls=%fused_computation.4 | convolution fusion | flops 1610612736 | bytes 14417920 | tf_op jit(solution)/shard_map/dot_general | solution.py:26
  47.0 9.7 %gather_tokens.3.both_ref = bf16[2,512,512]{2,1,0:T(8,128)(2,1)S(1)} custom-call(bf16[2,128,512]{2,1,0:T(8,128)(2,1)S(1)} %pad_maximum_fusion.own_ref), custom_call_target="tpu_custom_call" | custom-call | tf_op jit(solution)/shard_map/gather_tokens/pallas_call | solution.py:235
  56.8 18.4 %fast_step.3 = (bf16[4,128,1024]{2,1,0:T(8,128)(2,1)S(1)}, f32[512,768]{1,0:T(8,128)S(1)}, f32[512,768]{1,0:T(8,128)S(1)}, f32[512,768]{1,0:T(8,128)S(1)}) custom-call(s32[1]{0:T(128)} %bitcast.2.active_ref, bf16[2,512,512]{2,1,0:T(8,128)(2,1)S(1)} %gather_tokens.3.both_ref, bf16[128,512]{1,0:T(8,128)(2,1)S(1)} %multiply_convert_fusion.2.query_ref, ...), custom_call_target="tpu_custom_call" | custom-call | flops 10000000000 | bytes 20000000 | tf_op jit(solution)/shard_map/fast_step/pallas_call | solution.py:138
  75.2 1.2 copy-done.6
  76.4 37.8 %exchange.2 = (bf16[128,1024]{1,0:T(8,128)(2,1)S(1)}, bf16[128,4096]{1,0:T(8,128)(2,1)S(1)}) custom-call(bf16[4,128,1024]{2,1,0:T(8,128)(2,1)S(1)} %get-tuple-element.18.refs_0_, bf16[128,1024]{1,0:T(8,128)(2,1)S(1)} %get-tuple-element.38.refs_1_, bf16[128,1024]{1,0:T(8,128)(2,1)S(1)} %get-tuple-element.37.refs_2_), custom_call_target="tpu_custom_call" | custom-call | tf_op jit(solution)/shard_map/exchange/pallas_call | solution.py:470
  114.2 0.3 fusion.9
  114.5 8.9 %fusion.2 = f32[128,3,512]{2,0,1:T(8,128)S(1)} fusion(bf16[1,4096,1,3,512]{1,4,3,2,0:T(8,128)(2,1)} %copy.23, bf16[128,4096]{1,0:T(8,128)(2,1)S(1)} %get-tuple-element.19, f32[4096]{0:T(1024)S(1)} %bitcast.122, f32[128]{0:T(128)S(1)} %add_rsqrt_fusion.5), kind=kOutput, calls=%fused_computation.2 | convolution fusion | flops 1612709888 | bytes 14434816 | tf_op jit(solution)/shard_map/dot_general | solution.py:26
  123.9 8.7 %gather_tokens.4.both_ref = bf16[2,512,512]{2,1,0:T(8,128)(2,1)S(1)} custom-call(bf16[2,128,512]{2,1,0:T(8,128)(2,1)S(1)} %pad_maximum_fusion.1.own_ref), custom_call_target="tpu_custom_call" | custom-call | tf_op jit(solution)/shard_map/gather_tokens/pallas_call | solution.py:235
  132.6 18.4 %fast_step.4 = (bf16[4,128,1024]{2,1,0:T(8,128)(2,1)S(1)}, f32[512,768]{1,0:T(8,128)S(1)}, f32[512,768]{1,0:T(8,128)S(1)}, f32[512,768]{1,0:T(8,128)S(1)}) custom-call(s32[1]{0:T(128)} %bitcast.1.active_ref, bf16[2,512,512]{2,1,0:T(8,128)(2,1)S(1)} %gather_tokens.4.both_ref, bf16[128,512]{1,0:T(8,128)(2,1)S(1)} %multiply_convert_fusion.1.query_ref, ...), custom_call_target="tpu_custom_call" | custom-call | flops 10000000000 | bytes 20000000 | tf_op jit(solution)/shard_map/fast_step/pallas_call | solution.py:138
  151.0 37.6 %exchange.3 = (bf16[128,1024]{1,0:T(8,128)(2,1)S(1)}, bf16[128,4096]{1,0:T(8,128)(2,1)S(1)}) custom-call(bf16[4,128,1024]{2,1,0:T(8,128)(2,1)S(1)} %get-tuple-element.23.refs_0_, bf16[128,1024]{1,0:T(8,128)(2,1)S(1)} %constant_dynamic-slice_fusion.2.refs_1_, bf16[128,1024]{1,0:T(8,128)(2,1)S(1)} %get-tuple-element.37.refs_2_), custom_call_target="tpu_custom_call" | custom-call | tf_op jit(solution)/shard_map/exchange/pallas_call | solution.py:470
  188.6 0.3 fusion.12
  189.0 8.9 %fusion = f32[128,3,512]{2,0,1:T(8,128)S(1)} fusion(bf16[1,4096,1,3,512]{1,4,3,2,0:T(8,128)(2,1)} %copy.23, bf16[128,4096]{1,0:T(8,128)(2,1)S(1)} %get-tuple-element.24, f32[128]{0:T(128)S(1)} %add_rsqrt_fusion.2, f32[4096]{0:T(1024)S(1)} %bitcast.123), kind=kOutput, calls=%fused_computation | convolution fusion | flops 1612709888 | bytes 14434816 | tf_op jit(solution)/shard_map/dot_general | solution.py:26
  198.3 9.7 %gather_tokens.5.both_ref = bf16[2,512,512]{2,1,0:T(8,128)(2,1)S(1)} custom-call(bf16[2,128,512]{2,1,0:T(8,128)(2,1)S(1)} %pad_maximum_fusion.2.own_ref), custom_call_target="tpu_custom_call" | custom-call | tf_op jit(solution)/shard_map/gather_tokens/pallas_call | solution.py:235
  208.1 20.1 %fast_step.5 = (bf16[4,128,1024]{2,1,0:T(8,128)(2,1)S(1)}, f32[512,768]{1,0:T(8,128)}, f32[512,768]{1,0:T(8,128)}, f32[512,768]{1,0:T(8,128)}) custom-call(s32[1]{0:T(128)} %bitcast.active_ref, bf16[2,512,512]{2,1,0:T(8,128)(2,1)S(1)} %gather_tokens.5.both_ref, bf16[128,512]{1,0:T(8,128)(2,1)S(1)} %multiply_convert_fusion.query_ref, ...), custom_call_target="tpu_custom_call" | custom-call | flops 10000000000 | bytes 20000000 | tf_op jit(solution)/shard_map/fast_step/pallas_call | solution.py:138
  228.2 20.6 %reduce.10 = bf16[128,1024]{1,0:T(8,128)(2,1)S(1)} custom-call(bf16[4,128,1024]{2,1,0:T(8,128)(2,1)S(1)} %get-tuple-element.28.refs_0_, bf16[128,1024]{1,0:T(8,128)(2,1)S(1)} %constant_dynamic-slice_fusion.refs_1_), custom_call_target="tpu_custom_call" | custom-call | tf_op jit(solution)/shard_map/reduce/pallas_call | solution.py:470
  248.8 0.9 select_select_fusion
  (66 shorter events, 2.0 us)
Async XLA Ops:
  0.0 8.8 %copy-start.10 = (bf16[1,1,512,768]{3,2,1,0:T(8,128)(2,1)S(1)}, bf16[1,1,512,768]{3,2,1,0:T(8,128)(2,1)}, u32[]{:S(2)}) copy-start(bf16[1,1,512,768]{3,2,1,0:T(8,128)(2,1)} %param.14) | copy-start | bytes 2359300
  1.1 7.8 %copy-start.8 = (bf16[1,1,512,768]{3,2,1,0:T(8,128)(2,1)S(1)}, bf16[1,1,512,768]{3,2,1,0:T(8,128)(2,1)}, u32[]{:S(2)}) copy-start(bf16[1,1,512,768]{3,2,1,0:T(8,128)(2,1)} %param.15) | copy-start | bytes 2359300
  2.3 7.5 %copy-start.12 = (f32[1,4096]{1,0:T(1,128)S(1)}, f32[1,4096]{1,0:T(1,128)}, u32[]{:S(2)}) copy-start(f32[1,4096]{1,0:T(1,128)} %param.11) | copy-start | bytes 49156
  2.3 32.3 %all-to-all-start = ((bf16[4,128,1024]{2,1,0:T(8,128)(2,1)}), bf16[4,128,1024]{2,1,0:T(8,128)(2,1)}, u32[]{:S(2)}, u32[]{:S(2)}) async-start(bf16[4,128,1024]{2,1,0:T(8,128)(2,1)} %broadcast_in_dim.91), calls=%async_computation | async-start | bytes 2097152 | tf_op jit(solution)/shard_map/all_to_all | solution.py:488
  12.3 17.0 %copy-start.14 = (f32[1,2,128]{2,1,0:T(2,128)S(1)}, f32[1,2,128]{2,1,0:T(2,128)}, u32[]{:S(2)}) copy-start(f32[1,2,128]{2,1,0:T(2,128)} %param.17) | copy-start | bytes 3076
  12.4 17.0 %copy-start.13 = (f32[1,1,2,512]{3,2,1,0:T(2,128)S(1)}, f32[1,1,2,512]{3,2,1,0:T(2,128)}, u32[]{:S(2)}) copy-start(f32[1,1,2,512]{3,2,1,0:T(2,128)} %param.13) | copy-start | bytes 12292
  29.3 1.1 copy-start.9
  29.3 1.4 copy-start.11
  37.5 19.3 %copy-start.2 = (bf16[1,1,512,4096]{3,2,1,0:T(8,128)(2,1)S(1)}, bf16[1,1,512,4096]{3,2,1,0:T(8,128)(2,1)}, u32[]{:S(2)}) copy-start(bf16[1,1,512,4096]{3,2,1,0:T(8,128)(2,1)} %param.19) | copy-start | bytes 12582916
  46.5 10.2 %copy-start = (f32[512,768]{1,0:T(8,128)S(1)}, f32[512,768]{1,0:T(8,128)}, u32[]{:S(2)}) copy-start(f32[512,768]{1,0:T(8,128)} %get-tuple-element.44.up_ref) | copy-start | bytes 4718596
  46.5 10.2 %copy-start.1 = (f32[512,768]{1,0:T(8,128)S(1)}, f32[512,768]{1,0:T(8,128)}, u32[]{:S(2)}) copy-start(f32[512,768]{1,0:T(8,128)} %get-tuple-element.45.gate_ref) | copy-start | bytes 4718596
  46.6 10.2 %copy-start.3 = (f32[1,1,512]{2,1,0:T(1,128)S(1)}, f32[1,1,512]{2,1,0:T(1,128)}, u32[]{:S(2)}) copy-start(f32[1,1,512]{2,1,0:T(1,128)} %param.18) | copy-start | bytes 6148
  75.2 1.2 copy-start.6
  76.4 37.8 %copy-start.4 = (f32[512,768]{1,0:T(8,128)}, f32[512,768]{1,0:T(8,128)S(1)}, u32[]{:S(2)}) copy-start(f32[512,768]{1,0:T(8,128)S(1)} %get-tuple-element.21.up_ref) | copy-start | bytes 4718596
  123.3 9.2 %copy-start.5 = (f32[512,768]{1,0:T(8,128)S(1)}, f32[512,768]{1,0:T(8,128)}, u32[]{:S(2)}) copy-start(f32[512,768]{1,0:T(8,128)} %copy-done.4) | copy-start | bytes 4718596
  123.3 9.2 %copy-start.7 = (f32[512,768]{1,0:T(8,128)S(1)}, f32[512,768]{1,0:T(8,128)}, u32[]{:S(2)}) copy-start(f32[512,768]{1,0:T(8,128)} %copy-done.6) | copy-start | bytes 4718596
